TPU v7x, 32 devices: a whole 2x2x4 slice. The times are simulated.
32 devices in a mesh: dp: 4 (over z), ctx: 8 (over y, x, core).
Axes of the slice: x: 2, y: 2, z: 4, core: 2. Of those that a mesh axis runs over, the one named last changes fastest.
Arguments:
- patches: bfloat16 [8, 1024, 6144], P('dp', 'ctx'), may hold values from -6 to 6
- w_in: bfloat16 [6144, 768], P(('dp', 'ctx')), may hold values from -0.078125 to 0.078125
- b_in: bfloat16 [768], P(('dp', 'ctx')), may hold values from -3 to 3
- g_one: bfloat16 [768], P(('dp', 'ctx')), may hold values from 0.25 to 1.75
- s_one: bfloat16 [768], P(('dp', 'ctx')), may hold values from -3 to 3
- w_qkv: bfloat16 [768, 2304], P(('dp', 'ctx')), may hold values from -0.21875 to 0.21875
- w_out: bfloat16 [768, 768], P(('dp', 'ctx')), may hold values from -1.75 to 1.75
- b_out: bfloat16 [768], P(('dp', 'ctx')), may hold values from -3 to 3
- g_two: bfloat16 [768], P(('dp', 'ctx')), may hold values from 0.25 to 1.75
- s_two: bfloat16 [768], P(('dp', 'ctx')), may hold values from -3 to 3
- w_up: bfloat16 [768, 3072], P(('dp', 'ctx')), may hold values from -0.21875 to 0.21875
- b_up: bfloat16 [3072], P(('dp', 'ctx')), may hold values from -3 to 3
- w_down: bfloat16 [3072, 768], P(('dp', 'ctx')), may hold values from -0.109375 to 0.109375
- b_down: bfloat16 [768], P(('dp', 'ctx')), may hold values from -3 to 3
- cotangent: bfloat16 [8, 1024, 768], P('dp', 'ctx'), may hold values from -6 to 6
Outputs:
- block_out: bfloat16 [8, 1024, 768], P('dp', 'ctx')
- grad_patches: float32 [8, 1024, 6144], P('dp', 'ctx')
- grad_w_in: float32 [6144, 768], P(('dp', 'ctx'))
- grad_b_in: float32 [768], P(('dp', 'ctx'))
- grad_g_one: float32 [768], P(('dp', 'ctx'))
- grad_s_one: float32 [768], P(('dp', 'ctx'))
- grad_w_qkv: float32 [768, 2304], P(('dp', 'ctx'))
- grad_w_out: float32 [768, 768], P(('dp', 'ctx'))
- grad_b_out: float32 [768], P(('dp', 'ctx'))
- grad_g_two: float32 [768], P(('dp', 'ctx'))
- grad_s_two: float32 [768], P(('dp', 'ctx'))
- grad_w_up: float32 [768, 3072], P(('dp', 'ctx'))
- grad_b_up: float32 [3072], P(('dp', 'ctx'))
- grad_w_down: float32 [3072, 768], P(('dp', 'ctx'))
- grad_b_down: float32 [768], P(('dp', 'ctx'))
All inputs are finite; a program needn't handle non-finite values.
Results may differ from a plain program's by a relative error of at most 0.015.
Values may be sent and summed in bfloat16 or wider, within the bound.
No kernel may reach another device: no remote copies, remote signals or barrier semaphores. Data moves between devices by JAX's collectives and lax.ppermute only.
A program may use at most 256 MiB of HBM per device.

v0:
```python
import jax
import jax.numpy as jnp
from jax import lax
from jax.sharding import PartitionSpec as P

HEADS = 12
HEAD = 64


eps_norm = 1e-05
gelu_coef = 0.7978845608028654


def norm_forward(stream, gain, shift):
    row_mean = jnp.mean(stream, axis=-1, keepdims=True)
    centered = stream - row_mean
    variance = jnp.mean(centered * centered, axis=-1, keepdims=True)
    inverse = lax.rsqrt(variance + eps_norm)
    normed = centered * inverse
    return (normed * gain + shift, normed, inverse)


def norm_backward(upstream, normed, inverse, gain):
    scaled = upstream * gain
    row_inner = jnp.mean(scaled, axis=-1, keepdims=True)
    row_corr = jnp.mean(scaled * normed, axis=-1, keepdims=True)
    stream_grad = inverse * (scaled - row_inner - normed * row_corr)
    return (stream_grad, jnp.sum(upstream * normed, axis=0), jnp.sum(upstream, axis=0))


def gelu_pair(pre_act):
    tanh_val = jnp.tanh(gelu_coef * (pre_act + 0.044715 * pre_act * pre_act * pre_act))
    gelu_out = 0.5 * pre_act * (1.0 + tanh_val)
    gelu_slope = 0.5 * (1.0 + tanh_val) + 0.5 * pre_act * (
        1.0 - tanh_val * tanh_val
    ) * gelu_coef * (1.0 + 3.0 * 0.044715 * pre_act * pre_act)
    return (gelu_out, gelu_slope)


def block_scores(queries, kv_all, key_block, key_width, offset):
    model_width = queries.shape[1] * queries.shape[2]
    kv_piece = lax.dynamic_slice_in_dim(kv_all, key_block * key_width, key_width, 0)
    key_rows = kv_piece[:, :model_width].reshape(key_width, HEADS, HEAD)
    value_rows = kv_piece[:, model_width:].reshape(key_width, HEADS, HEAD)
    scores = (
        jnp.einsum("qhd,khd->hqk", queries, key_rows, preferred_element_type=jnp.float32) * 0.125
    )
    key_pos = key_block * key_width + lax.iota(jnp.int32, key_width)
    row_pos = offset + lax.iota(jnp.int32, queries.shape[0])
    allowed = key_pos[None, :] <= row_pos[:, None]
    return (jnp.where(allowed[None], scores, -1e30), key_rows, value_rows)


def log_totals(queries, kv_all, key_width, offset, last_block):
    row_shape = (HEADS, queries.shape[0])

    def lse_step(key_block, state_pair):
        row_top, row_total = state_pair
        scores, key_rows, value_rows = block_scores(queries, kv_all, key_block, key_width, offset)
        new_top = jnp.maximum(row_top, jnp.max(scores, axis=-1))
        row_total = row_total * jnp.exp(row_top - new_top) + jnp.sum(
            jnp.exp(scores - new_top[..., None]), axis=-1
        )
        return (new_top, row_total)

    start_pair = (jnp.full(row_shape, -1e30, jnp.float32), jnp.zeros(row_shape, jnp.float32))
    row_top, row_total = lax.fori_loop(0, last_block, lse_step, start_pair)
    return row_top + jnp.log(row_total)


def attend_rows(queries, kv_all, row_lse, key_width, offset, last_block):

    def out_step(key_block, accumulated):
        scores, key_rows, value_rows = block_scores(queries, kv_all, key_block, key_width, offset)
        attn_probs = jnp.exp(scores - row_lse[..., None]).astype(jnp.bfloat16)
        return accumulated + jnp.einsum(
            "hqk,khd->qhd", attn_probs, value_rows, preferred_element_type=jnp.float32
        )

    accumulated = lax.fori_loop(0, last_block, out_step, jnp.zeros(queries.shape, jnp.float32))
    return accumulated.reshape(queries.shape[0], -1).astype(jnp.bfloat16)


def delta_rows(queries, kv_all, row_lse, grad_rows, key_width, offset, last_block):

    def delta_step(key_block, row_delta):
        scores, key_rows, value_rows = block_scores(queries, kv_all, key_block, key_width, offset)
        plain_probs = jnp.exp(scores - row_lse[..., None])
        prob_grad = jnp.einsum(
            "qhd,khd->hqk", grad_rows, value_rows, preferred_element_type=jnp.float32
        )
        return row_delta + jnp.sum(plain_probs * prob_grad, axis=-1)

    return lax.fori_loop(0, last_block, delta_step, jnp.zeros(row_lse.shape, jnp.float32))


def attend_back(
    queries, kv_all, row_lse, row_delta, grad_rows, key_width, offset, last_block, length
):
    model_width = queries.shape[1] * queries.shape[2]

    def grad_step(key_block, state_pair):
        query_grad, kv_grad = state_pair
        scores, key_rows, value_rows = block_scores(queries, kv_all, key_block, key_width, offset)
        plain_probs = jnp.exp(scores - row_lse[..., None])
        prob_grad = jnp.einsum(
            "qhd,khd->hqk", grad_rows, value_rows, preferred_element_type=jnp.float32
        )
        score_grad = (plain_probs * (prob_grad - row_delta[..., None])).astype(jnp.bfloat16)
        query_grad = query_grad + jnp.einsum(
            "hqk,khd->qhd", score_grad, key_rows, preferred_element_type=jnp.float32
        )
        key_grad = (
            jnp.einsum("hqk,qhd->khd", score_grad, queries, preferred_element_type=jnp.float32)
            * 0.125
        )
        value_grad = jnp.einsum(
            "hqk,qhd->khd",
            plain_probs.astype(jnp.bfloat16),
            grad_rows,
            preferred_element_type=jnp.float32,
        )
        kv_piece = jnp.concatenate(
            [key_grad.reshape(key_width, -1), value_grad.reshape(key_width, -1)], axis=1
        )
        kv_grad = lax.dynamic_update_slice_in_dim(kv_grad, kv_piece, key_block * key_width, 0)
        return (query_grad, kv_grad)

    start_pair = (
        jnp.zeros(queries.shape, jnp.float32),
        jnp.zeros((length, 2 * model_width), jnp.float32),
    )
    query_grad, kv_grad = lax.fori_loop(0, last_block, grad_step, start_pair)
    return (query_grad.reshape(queries.shape[0], -1) * 0.125, kv_grad)


def per_device(
    patches,
    w_in,
    b_in,
    g_one,
    s_one,
    w_qkv,
    w_out,
    b_out,
    g_two,
    s_two,
    w_up,
    b_up,
    w_down,
    b_down,
    cotangent,
):
    shards = (
        w_in,
        b_in,
        g_one,
        s_one,
        w_qkv,
        w_out,
        b_out,
        g_two,
        s_two,
        w_up,
        b_up,
        w_down,
        b_down,
    )
    micro_count = patches.shape[0]
    row_count = patches.shape[1]
    model_width = w_qkv.shape[1] // 3
    all_devices = lax.axis_size(("dp", "ctx"))
    length = row_count * lax.axis_size("ctx")
    key_width = min(512, length)
    offset = lax.axis_index("ctx") * row_count
    last_block = (offset + row_count - 1) // key_width + 1
    totals = [
        jnp.zeros((shard.shape[0] * all_devices,) + shard.shape[1:], jnp.float32)
        for shard in shards
    ]
    outputs = []
    in_grads = []
    for batch_index in range(micro_count):
        gathered = (
            lax.all_gather(w_in, ("dp", "ctx"), axis=0, tiled=True),
            lax.all_gather(b_in, ("dp", "ctx"), axis=0, tiled=True),
            lax.all_gather(g_one, ("dp", "ctx"), axis=0, tiled=True),
            lax.all_gather(s_one, ("dp", "ctx"), axis=0, tiled=True),
            lax.all_gather(w_qkv, ("dp", "ctx"), axis=0, tiled=True),
            lax.all_gather(w_out, ("dp", "ctx"), axis=0, tiled=True),
            lax.all_gather(b_out, ("dp", "ctx"), axis=0, tiled=True),
            lax.all_gather(g_two, ("dp", "ctx"), axis=0, tiled=True),
            lax.all_gather(s_two, ("dp", "ctx"), axis=0, tiled=True),
            lax.all_gather(w_up, ("dp", "ctx"), axis=0, tiled=True),
            lax.all_gather(b_up, ("dp", "ctx"), axis=0, tiled=True),
            lax.all_gather(w_down, ("dp", "ctx"), axis=0, tiled=True),
            lax.all_gather(b_down, ("dp", "ctx"), axis=0, tiled=True),
        )
        seq_patches = patches[batch_index]
        h_zero = jnp.dot(seq_patches, gathered[0], preferred_element_type=jnp.float32) + gathered[
            1
        ].astype(jnp.float32)
        gain_one = gathered[2].astype(jnp.float32)
        n_one, normed_one, inverse_one = norm_forward(
            h_zero, gain_one, gathered[3].astype(jnp.float32)
        )
        a_one = n_one.astype(jnp.bfloat16)
        projected = jnp.dot(a_one, gathered[4], preferred_element_type=jnp.float32).astype(
            jnp.bfloat16
        )
        queries = projected[:, :model_width].reshape(row_count, HEADS, HEAD)
        kv_all = lax.all_gather(projected[:, model_width:], "ctx", axis=0, tiled=True)
        row_lse = log_totals(queries, kv_all, key_width, offset, last_block)
        attended = attend_rows(queries, kv_all, row_lse, key_width, offset, last_block)
        h_one = (
            h_zero
            + jnp.dot(attended, gathered[5], preferred_element_type=jnp.float32)
            + gathered[6].astype(jnp.float32)
        )
        gain_two = gathered[7].astype(jnp.float32)
        n_two, normed_two, inverse_two = norm_forward(
            h_one, gain_two, gathered[8].astype(jnp.float32)
        )
        a_two = n_two.astype(jnp.bfloat16)
        pre_act = jnp.dot(a_two, gathered[9], preferred_element_type=jnp.float32) + gathered[
            10
        ].astype(jnp.float32)
        gelu_out, gelu_slope = gelu_pair(pre_act)
        hidden = gelu_out.astype(jnp.bfloat16)
        result = (
            h_one
            + jnp.dot(hidden, gathered[11], preferred_element_type=jnp.float32)
            + gathered[12].astype(jnp.float32)
        )
        outputs.append(result.astype(jnp.bfloat16))
        back_weights = (
            lax.all_gather(w_in, ("dp", "ctx"), axis=0, tiled=True),
            lax.all_gather(b_in, ("dp", "ctx"), axis=0, tiled=True),
            lax.all_gather(g_one, ("dp", "ctx"), axis=0, tiled=True),
            lax.all_gather(s_one, ("dp", "ctx"), axis=0, tiled=True),
            lax.all_gather(w_qkv, ("dp", "ctx"), axis=0, tiled=True),
            lax.all_gather(w_out, ("dp", "ctx"), axis=0, tiled=True),
            lax.all_gather(b_out, ("dp", "ctx"), axis=0, tiled=True),
            lax.all_gather(g_two, ("dp", "ctx"), axis=0, tiled=True),
            lax.all_gather(s_two, ("dp", "ctx"), axis=0, tiled=True),
            lax.all_gather(w_up, ("dp", "ctx"), axis=0, tiled=True),
            lax.all_gather(b_up, ("dp", "ctx"), axis=0, tiled=True),
            lax.all_gather(w_down, ("dp", "ctx"), axis=0, tiled=True),
            lax.all_gather(b_down, ("dp", "ctx"), axis=0, tiled=True),
        )
        seq_cot = cotangent[batch_index]
        cot_float = seq_cot.astype(jnp.float32)
        totals[12] = totals[12] + jnp.sum(cot_float, axis=0)
        totals[11] = totals[11] + jnp.dot(hidden.T, seq_cot, preferred_element_type=jnp.float32)
        pre_grad = (
            jnp.dot(seq_cot, back_weights[11].T, preferred_element_type=jnp.float32) * gelu_slope
        )
        totals[10] = totals[10] + jnp.sum(pre_grad, axis=0)
        up_grad = pre_grad.astype(jnp.bfloat16)
        totals[9] = totals[9] + jnp.dot(a_two.T, up_grad, preferred_element_type=jnp.float32)
        two_grad = jnp.dot(up_grad, back_weights[9].T, preferred_element_type=jnp.float32)
        norm_grad, gain_grad, shift_grad = norm_backward(
            two_grad, normed_two, inverse_two, back_weights[7].astype(jnp.float32)
        )
        totals[7] = totals[7] + gain_grad
        totals[8] = totals[8] + shift_grad
        stream_one = cot_float + norm_grad
        totals[6] = totals[6] + jnp.sum(stream_one, axis=0)
        out_grad = stream_one.astype(jnp.bfloat16)
        totals[5] = totals[5] + jnp.dot(attended.T, out_grad, preferred_element_type=jnp.float32)
        attended_grad = jnp.dot(
            out_grad, back_weights[5].T, preferred_element_type=jnp.float32
        ).astype(jnp.bfloat16)
        grad_rows = attended_grad.reshape(row_count, HEADS, HEAD)
        row_delta = delta_rows(queries, kv_all, row_lse, grad_rows, key_width, offset, last_block)
        query_grad, kv_terms = attend_back(
            queries, kv_all, row_lse, row_delta, grad_rows, key_width, offset, last_block, length
        )
        kv_local = lax.psum_scatter(
            kv_terms.astype(jnp.bfloat16), "ctx", scatter_dimension=0, tiled=True
        ).astype(jnp.float32)
        projected_grad = jnp.concatenate([query_grad, kv_local], axis=1).astype(jnp.bfloat16)
        totals[4] = totals[4] + jnp.dot(a_one.T, projected_grad, preferred_element_type=jnp.float32)
        one_grad = jnp.dot(projected_grad, back_weights[4].T, preferred_element_type=jnp.float32)
        norm_grad, gain_grad, shift_grad = norm_backward(
            one_grad, normed_one, inverse_one, back_weights[2].astype(jnp.float32)
        )
        totals[2] = totals[2] + gain_grad
        totals[3] = totals[3] + shift_grad
        stream_zero = stream_one + norm_grad
        totals[1] = totals[1] + jnp.sum(stream_zero, axis=0)
        zero_grad = stream_zero.astype(jnp.bfloat16)
        totals[0] = totals[0] + jnp.dot(
            seq_patches.T, zero_grad, preferred_element_type=jnp.float32
        )
        in_grads.append(jnp.dot(zero_grad, back_weights[0].T, preferred_element_type=jnp.float32))
    owned = (
        lax.psum_scatter(totals[0], ("dp", "ctx"), scatter_dimension=0, tiled=True),
        lax.psum_scatter(totals[1], ("dp", "ctx"), scatter_dimension=0, tiled=True),
        lax.psum_scatter(totals[2], ("dp", "ctx"), scatter_dimension=0, tiled=True),
        lax.psum_scatter(totals[3], ("dp", "ctx"), scatter_dimension=0, tiled=True),
        lax.psum_scatter(totals[4], ("dp", "ctx"), scatter_dimension=0, tiled=True),
        lax.psum_scatter(totals[5], ("dp", "ctx"), scatter_dimension=0, tiled=True),
        lax.psum_scatter(totals[6], ("dp", "ctx"), scatter_dimension=0, tiled=True),
        lax.psum_scatter(totals[7], ("dp", "ctx"), scatter_dimension=0, tiled=True),
        lax.psum_scatter(totals[8], ("dp", "ctx"), scatter_dimension=0, tiled=True),
        lax.psum_scatter(totals[9], ("dp", "ctx"), scatter_dimension=0, tiled=True),
        lax.psum_scatter(totals[10], ("dp", "ctx"), scatter_dimension=0, tiled=True),
        lax.psum_scatter(totals[11], ("dp", "ctx"), scatter_dimension=0, tiled=True),
        lax.psum_scatter(totals[12], ("dp", "ctx"), scatter_dimension=0, tiled=True),
    )
    return (jnp.stack(outputs), jnp.stack(in_grads)) + tuple(owned)


def solution(mesh):
    placed = (
        P("dp", "ctx", None),
        P(("dp", "ctx"), None),
        P(("dp", "ctx")),
        P(("dp", "ctx")),
        P(("dp", "ctx")),
        P(("dp", "ctx"), None),
        P(("dp", "ctx"), None),
        P(("dp", "ctx")),
        P(("dp", "ctx")),
        P(("dp", "ctx")),
        P(("dp", "ctx"), None),
        P(("dp", "ctx")),
        P(("dp", "ctx"), None),
        P(("dp", "ctx")),
        P("dp", "ctx", None),
    )
    return jax.shard_map(
        per_device,
        mesh=mesh,
        in_specs=placed,
        out_specs=(
            P("dp", "ctx", None),
            P("dp", "ctx", None),
            P(("dp", "ctx"), None),
            P(("dp", "ctx")),
            P(("dp", "ctx")),
            P(("dp", "ctx")),
            P(("dp", "ctx"), None),
            P(("dp", "ctx"), None),
            P(("dp", "ctx")),
            P(("dp", "ctx")),
            P(("dp", "ctx")),
            P(("dp", "ctx"), None),
            P(("dp", "ctx")),
            P(("dp", "ctx"), None),
            P(("dp", "ctx")),
        ),
        check_vma=False,
    )
```

profile of v0, /device:TPU:0, one launch (start us, length us, event | category | flops | bytes accessed | tf_op | source)
XLA Modules:
  0.0 1311.8 jit_solution(26952344656384240)
XLA Ops:
  15.4 42.9 %all-reduce.17 = (bf16[768]{0:T(1024)(128)(2,1)S(1)}, bf16[768]{0:T(1024)(128)(2,1)S(1)}, bf16[768]{0:T(1024)(128)(2,1)S(1)}, bf16[768]{0:T(1024)(128)(2,1)}, bf...) all-reduce(bf16[768]{0:T(1024)(128)(2,1)S(1)} %dynamic-update-slice, ...), channel_id=1, replica_groups=mesh['dp'=4,'ctx'=8] {'dp','ctx'}, use_global_device_ids=true, to_apply=%add | all-reduce | flops 8448 | bytes 33792
  58.3 37.5 %all-gather.8.cloned.1.call-done = bf16[6144,768]{1,0:T(8,128)(2,1)} async-done(((bf16[192,768]{1,0:T(8,128)(2,1)}), bf16[6144,768]{1,0:T(8,128)(2,1)}) %all-gather.8.cloned.1.call-update) | async-done | bytes 9437200 | tf_op jit(solution)/shard_map/all_gather | solution.py:185
  95.8 5.6 fusion.127
  101.7 55.7 %all-gather.10.cloned.1.call-done = bf16[768,2304]{1,0:T(8,128)(2,1)} async-done(((bf16[24,2304]{1,0:T(8,128)(2,1)}), bf16[768,2304]{1,0:T(8,128)(2,1)}) %all-gather.10.cloned.1.call-update) | async-done | bytes 3538960 | tf_op jit(solution)/shard_map/all_gather | solution.py:189
  157.4 2.7 convolution_convert_fusion.1
  161.7 5.8 fusion.125
  177.6 15.4 %all-gather.12.cloned.1.call-done = bf16[1024,1536]{1,0:T(8,128)(2,1)} async-done(((bf16[128,1536]{1,0:T(8,128)(2,1)}), bf16[1024,1536]{1,0:T(8,128)(2,1)}) %all-gather.12.cloned.1.call-update) | async-done | bytes 3145744 | tf_op jit(solution)/shard_map/all_gather | solution.py:212
  193.0 3.2 copy.86
  201.2 5.6 while.89
  203.3 3.5 fusion.267
  208.5 18.6 %all-gather.20.cloned.1.call-done = bf16[1024,1536]{1,0:T(8,128)(2,1)} async-done(((bf16[128,1536]{1,0:T(8,128)(2,1)}), bf16[1024,1536]{1,0:T(8,128)(2,1)}) %all-gather.20.cloned.1.call-update) | async-done | bytes 3145744 | tf_op jit(solution)/shard_map/all_gather | solution.py:212
  227.1 4.6 copy.89
  232.3 3.7 while.90
  238.1 7.0 while.91
  238.9 2.7 constant_dynamic-slice_fusion.15
  241.5 3.5 fusion.274
  246.8 37.1 %all-gather.14.cloned.1.call-done = bf16[768,768]{1,0:T(8,128)(2,1)} async-done(((bf16[24,768]{1,0:T(8,128)(2,1)}), bf16[768,768]{1,0:T(8,128)(2,1)}) %all-gather.14.cloned.1.call-update) | async-done | bytes 1179664 | tf_op jit(solution)/shard_map/all_gather | solution.py:190
  289.6 59.6 %all-gather.16.cloned.1.call-done = bf16[768,3072]{1,0:T(8,128)(2,1)} async-done(((bf16[24,3072]{1,0:T(8,128)(2,1)}), bf16[768,3072]{1,0:T(8,128)(2,1)}) %all-gather.16.cloned.1.call-update) | async-done | bytes 4718608 | tf_op jit(solution)/shard_map/all_gather | solution.py:194
  349.2 4.5 convolution_add_fusion.3
  353.7 60.9 %all-gather.18.cloned.1.call-done = bf16[3072,768]{1,0:T(8,128)(2,1)} async-done(((bf16[96,768]{1,0:T(8,128)(2,1)}), bf16[3072,768]{1,0:T(8,128)(2,1)}) %all-gather.18.cloned.1.call-update) | async-done | bytes 4718608 | tf_op jit(solution)/shard_map/all_gather | solution.py:196
  414.6 5.5 fusion.130
  423.7 2.5 fusion.129
  434.0 2.6 convolution_convert_fusion.2
  438.4 3.6 while.94
  442.6 11.3 while.92
  456.8 7.4 while.93
  464.3 4.7 copy.105
  471.9 7.4 while.95
  479.3 4.6 copy.107
  489.4 5.5 convolution_add_fusion.1
  497.8 5.0 convolution_add_fusion.2
  504.2 23.9 %reduce-scatter.22.cloned.1.call-done = bf16[128,1536]{1,0:T(8,128)(2,1)} async-done(((bf16[1024,1536]{1,0:T(8,128)(2,1)}), bf16[128,1536]{1,0:T(8,128)(2,1)}) %reduce-scatter.22.cloned.1.call-update) | async-done | bytes 393232
  529.3 49.4 %reduce-scatter.24.cloned.1.call-done = bf16[128,1536]{1,0:T(8,128)(2,1)} async-done(((bf16[1024,1536]{1,0:T(8,128)(2,1)}), bf16[128,1536]{1,0:T(8,128)(2,1)}) %reduce-scatter.24.cloned.1.call-update) | async-done | bytes 393232
  581.3 4.1 convolution_add_fusion
  587.5 3.4 multiply_reduce_fusion.3
  593.0 8.1 fusion.63
  601.1 12.6 add_bitcast_fusion
  613.7 18.7 %copy.109 = f32[6144,768]{1,0:T(8,128)} copy(f32[6144,768]{0,1:T(8,128)} %add_bitcast_fusion) | data formatting | bytes 37748736
  634.0 3.5 fusion.83
  637.6 3.5 fusion.84
  642.0 40.9 %all-reduce.16 = (f32[768]{0:T(1024)S(1)}, f32[768]{0:T(1024)S(1)}, f32[768]{0:T(1024)S(1)}, f32[768]{0:T(1024)S(1)}, f32[768]{0:T(1024)S(1)}, /*index=5*/f32[76...) all-reduce(f32[768]{0:T(1024)S(1)} %add.529, ...), channel_id=5, replica_groups=mesh['dp'=4,'ctx'=8] {'dp','ctx'}, use_global_device_ids=true, to_apply=%region_43.44.clone | all-reduce | flops 8448 | bytes 67584
  687.6 6.9 convolution_bitcast_fusion.2
  694.5 3.1 convolution_bitcast_fusion.3
  697.6 3.1 pad_maximum_fusion
  700.8 125.0 %reduce-scatter.20.cloned.1.call-done = f32[96,768]{1,0:T(8,128)} async-done(((f32[3072,768]{1,0:T(8,128)}), f32[96,768]{1,0:T(8,128)}) %reduce-scatter.20.cloned.1.call-update) | async-done | bytes 294928 | tf_op jit(solution)/shard_map/reduce_scatter | solution.py:309
  825.8 140.9 %reduce-scatter.18.cloned.1.call-done = f32[24,3072]{1,0:T(8,128)} async-done(((f32[768,3072]{1,0:T(8,128)}), f32[24,3072]{1,0:T(8,128)}) %reduce-scatter.18.cloned.1.call-update) | async-done | bytes 294928 | tf_op jit(solution)/shard_map/reduce_scatter | solution.py:307
  966.7 125.3 %reduce-scatter.14.cloned.1.call-done = f32[24,2304]{1,0:T(8,128)} async-done(((f32[768,2304]{1,0:T(8,128)}), f32[24,2304]{1,0:T(8,128)}) %reduce-scatter.14.cloned.1.call-update) | async-done | bytes 221200 | tf_op jit(solution)/shard_map/reduce_scatter | solution.py:302
  1092.0 212.8 %reduce-scatter.26.cloned.1.call-done = f32[192,768]{1,0:T(8,128)} async-done(((f32[6144,768]{1,0:T(8,128)}), f32[192,768]{1,0:T(8,128)}) %reduce-scatter.26.cloned.1.call-update) | async-done | bytes 589840
  (431 shorter events, 109.9 us)
Async XLA Ops:
  7.2 88.6 %all-gather.8.cloned.1.call-start = ((), (), s32[]{:S(2)}) async-start(), calls=%async_computation.7 | async-start | bytes 9732096 | tf_op jit(solution)/shard_map/all_gather | solution.py:185
  7.9 149.5 %all-gather.10.cloned.1.call-start = ((), (), s32[]{:S(2)}) async-start(), calls=%async_computation.8 | async-start | bytes 3649536 | tf_op jit(solution)/shard_map/all_gather | solution.py:189
  8.7 184.3 %all-gather.12.cloned.1.call-start = ((), (), s32[]{:S(2)}) async-start(), calls=%async_computation.9 | async-start | bytes 3538944 | tf_op jit(solution)/shard_map/all_gather | solution.py:212
  58.3 109.4 %copy-start.59 = (f32[768]{0:T(1024)}, f32[768]{0:T(1024)S(1)}, u32[]{:S(2)}) copy-start(f32[768]{0:T(1024)S(1)} %convert_element_type.137) | copy-start | bytes 9220
  58.3 109.4 %copy-start.68 = (f32[768]{0:T(1024)}, f32[768]{0:T(1024)S(1)}, u32[]{:S(2)}) copy-start(f32[768]{0:T(1024)S(1)} %convert_element_type.138) | copy-start | bytes 9220
  101.4 60.2 %copy-start.16 = (f32[128,768]{1,0:T(8,128)}, f32[128,768]{1,0:T(8,128)S(1)}, u32[]{:S(2)}) copy-start(f32[128,768]{1,0:T(8,128)S(1)} %get-tuple-element.817) | copy-start | bytes 1179652
  101.4 60.2 %copy-start.93 = (f32[128]{0:T(128)}, f32[128]{0:T(128)S(1)}, u32[]{:S(2)}) copy-start(f32[128]{0:T(128)S(1)} %broadcast_multiply_fusion.11) | copy-start | bytes 1540
  101.7 60.0 %copy-start.108 = (f32[128]{0:T(128)}, f32[128]{0:T(128)S(1)}, u32[]{:S(2)}) copy-start(f32[128]{0:T(128)S(1)} %add_rsqrt_fusion.3) | copy-start | bytes 1540
  161.7 6.1 copy-start.2
  161.7 65.4 %all-gather.20.cloned.1.call-start = ((), (), s32[]{:S(2)}) async-start(), calls=%async_computation.13 | async-start | bytes 3538944 | tf_op jit(solution)/shard_map/all_gather | solution.py:212
  170.2 113.7 %all-gather.14.cloned.1.call-start = ((), (), s32[]{:S(2)}) async-start(), calls=%async_computation.10 | async-start | bytes 1216512 | tf_op jit(solution)/shard_map/all_gather | solution.py:190
  170.7 178.5 %all-gather.16.cloned.1.call-start = ((), (), s32[]{:S(2)}) async-start(), calls=%async_computation.11 | async-start | bytes 4866048 | tf_op jit(solution)/shard_map/all_gather | solution.py:194
  171.3 243.3 %all-gather.18.cloned.1.call-start = ((), (), s32[]{:S(2)}) async-start(), calls=%async_computation.12 | async-start | bytes 4866048 | tf_op jit(solution)/shard_map/all_gather | solution.py:196
  172.1 356.0 %reduce-scatter.22.cloned.1.call-start = ((), (), s32[]{:S(2)}) async-start(), calls=%async_computation.18 | async-start | bytes 3538944
  238.1 45.8 %copy-start.75 = (f32[768]{0:T(1024)S(1)}, f32[768]{0:T(1024)}, u32[]{:S(2)}) copy-start(f32[768]{0:T(1024)} %convert_element_type.143) | copy-start | bytes 9220
  285.9 142.7 %copy-start.76 = (f32[128]{0:T(128)}, f32[128]{0:T(128)S(1)}, u32[]{:S(2)}) copy-start(f32[128]{0:T(128)S(1)} %broadcast_multiply_fusion.10) | copy-start | bytes 1540
  287.7 140.9 %copy-start.86 = (f32[128]{0:T(128)}, f32[128]{0:T(128)S(1)}, u32[]{:S(2)}) copy-start(f32[128]{0:T(128)S(1)} %broadcast_multiply_fusion.8) | copy-start | bytes 1540
  414.6 6.4 copy-start.1
  414.6 9.0 slice-start.3
  469.0 109.7 %reduce-scatter.24.cloned.1.call-start = ((), (), s32[]{:S(2)}) async-start(), calls=%async_computation.19 | async-start | bytes 3538944
  484.0 216.8 %reduce-scatter.16.cloned.1.call-start = ((), (), s32[]{:S(2)}) async-start(), calls=%async_computation.15 | async-start | bytes 2433024 | tf_op jit(solution)/shard_map/reduce_scatter | solution.py:303
  487.6 338.2 %reduce-scatter.20.cloned.1.call-start = ((), (), s32[]{:S(2)}) async-start(), calls=%async_computation.17 | async-start | bytes 9732096 | tf_op jit(solution)/shard_map/reduce_scatter | solution.py:309
  495.0 471.7 %reduce-scatter.18.cloned.1.call-start = ((), (), s32[]{:S(2)}) async-start(), calls=%async_computation.16 | async-start | bytes 9732096 | tf_op jit(solution)/shard_map/reduce_scatter | solution.py:307
  502.8 77.1 %copy-start.60 = (f32[768]{0:T(1024)S(1)}, f32[768]{0:T(1024)}, u32[]{:S(2)}) copy-start(f32[768]{0:T(1024)} %copy-done.59) | copy-start | bytes 9220
  502.8 77.1 %copy-start.69 = (f32[768]{0:T(1024)S(1)}, f32[768]{0:T(1024)}, u32[]{:S(2)}) copy-start(f32[768]{0:T(1024)} %copy-done.68) | copy-start | bytes 9220
  502.8 77.1 %copy-start.94 = (f32[128]{0:T(128)S(1)}, f32[128]{0:T(128)}, u32[]{:S(2)}) copy-start(f32[128]{0:T(128)} %copy-done.93) | copy-start | bytes 1540
  502.8 77.1 %copy-start.109 = (f32[128]{0:T(128)S(1)}, f32[128]{0:T(128)}, u32[]{:S(2)}) copy-start(f32[128]{0:T(128)} %copy-done.108) | copy-start | bytes 1540
  502.9 77.1 %copy-start.17 = (f32[128,768]{1,0:T(8,128)S(1)}, f32[128,768]{1,0:T(8,128)}, u32[]{:S(2)}) copy-start(f32[128,768]{1,0:T(8,128)} %copy-done.16) | copy-start | bytes 1179652
  502.9 589.1 %reduce-scatter.14.cloned.1.call-start = ((), (), s32[]{:S(2)}) async-start(), calls=%async_computation.14 | async-start | bytes 7299072 | tf_op jit(solution)/shard_map/reduce_scatter | solution.py:302
  504.0 77.3 %copy-start.58 = (bf16[128,12,64]{0,2,1:T(8,128)(2,1)}, bf16[128,12,64]{0,2,1:T(8,128)(2,1)S(1)}, u32[]{:S(2)}) copy-start(bf16[128,12,64]{0,2,1:T(8,128)(2,1)S(1)} %multiply_convert_fusion.3) | copy-start | bytes 589828
  504.2 77.1 %copy-start.51 = (bf16[128,12,64]{0,2,1:T(8,128)(2,1)}, bf16[128,12,64]{0,2,1:T(8,128)(2,1)S(1)}, u32[]{:S(2)}) copy-start(bf16[128,12,64]{0,2,1:T(8,128)(2,1)S(1)} %multiply_convert_fusion.2) | copy-start | bytes 589828
  529.3 52.0 %copy-start.57 = (bf16[128,1536]{0,1:T(8,128)(2,1)}, bf16[128,1536]{0,1:T(8,128)(2,1)S(1)}, u32[]{:S(2)}) copy-start(bf16[128,1536]{0,1:T(8,128)(2,1)S(1)} %copy.106) | copy-start | bytes 1179652
  585.5 719.4 %reduce-scatter.26.cloned.1.call-start = ((), (), s32[]{:S(2)}) async-start(), calls=%async_computation.20 | async-start | bytes 19464192
  587.4 3.4 copy-start.42
  587.4 3.4 copy-start.52
  587.5 3.4 copy-start.90
  587.5 3.4 copy-start.95
  587.5 3.4 copy-start.102
  587.5 3.4 copy-start.110
  592.4 8.7 copy-start.47
  634.0 3.5 copy-start.22
  634.0 3.5 copy-start.33
  637.6 4.3 copy-start.112
  637.6 4.3 copy-start.111
  637.6 56.9 %slice-start = ((s8[9437184]{0:T(1024)(128)(4,1)}), s8[1048576]{0:T(1024)(128)(4,1)S(1)}, s32[]{:S(2)}) async-start(s8[9437184]{0:T(1024)(128)(4,1)} %bitcast.411), calls=%async_computation.21 | async-start | bytes 2097152
  687.6 6.9 slice-start.1
  687.6 6.9 slice-start.2
  687.6 7.0 copy-start.48
  (85 other events, 130.3 us)
Sparse Core Ops, SparseCore 0:
  10.9 84.8 all-gather.7
  98.7 58.6 all-gather.9
  161.8 31.1 all-gather.11
  194.7 32.3 all-gather.19
  229.8 54.0 all-gather.13
  286.6 62.5 all-gather.15
  352.1 62.4 all-gather.17
  469.1 58.9 reduce-scatter.21
  532.4 46.2 reduce-scatter.23
  584.4 99.1 reduce-scatter.15
  691.0 134.6 reduce-scatter.19
  832.1 134.5 reduce-scatter.17
  973.9 118.0 reduce-scatter.13
  1098.8 205.9 reduce-scatter.25
where the time goes:
time: 1320 us; the launch traced here: 1310 us
  waiting for transfers between devices  965 us (73%)
  matrix products  124 us (9%)
  local copies, waits for them, and re-layouts  91.7 us (7%)
  blocking collectives  83.8 us (6%)
  other arithmetic  21.3 us (2%)
  between operations  15.7 us (1%)
    unnamed x17, waiting for transfers between devices  289 us
    reduce_scatter x1, waiting for transfers between devices, per_device(): lax.psum_scatter(totals[9], ('dp', 'ctx'), scatter_dimension=0, tiled=True)  141 us
    reduce_scatter x1, waiting for transfers between devices, per_device(): lax.psum_scatter(totals[4], ('dp', 'ctx'), scatter_dimension=0, tiled=True)  125 us
    reduce_scatter x1, waiting for transfers between devices, per_device(): lax.psum_scatter(totals[11], ('dp', 'ctx'), scatter_dimension=0, tiled=True)  125 us
    unnamed x2, blocking collectives  83.8 us
    all_gather x1, waiting for transfers between devices, per_device(): lax.all_gather(w_down, ('dp', 'ctx'), axis=0, tiled=True)  60.9 us
    all_gather x1, waiting for transfers between devices, per_device(): lax.all_gather(w_up, ('dp', 'ctx'), axis=0, tiled=True)  59.6 us
    all_gather x1, waiting for transfers between devices, per_device(): lax.all_gather(w_qkv, ('dp', 'ctx'), axis=0, tiled=True)  55.7 us
  transfers between devices with their start and end apart: 14, of which 13 were waited for; matrix products, arithmetic and copies ran while one was open for 13% of the time, Pallas kernels for 0%

commit v1 on v0

v1 whole, which is shorter than its diff:
```python
import math

import jax
import jax.numpy as jnp
import numpy as np
from jax import lax
from jax.experimental import pallas as pl
from jax.experimental.pallas import tpu as pltpu
from jax.sharding import Mesh
from jax.sharding import PartitionSpec as P

HEADS = 12
HEAD = 64

eps_norm = 1e-05
gelu_coef = 0.7978845608028654
PLANE = ("y", "x", "c")
ALL = ("z", "y", "x", "c")
bf16 = jnp.bfloat16
f32 = jnp.float32


def norm_forward(stream, gain, shift):
    row_mean = jnp.mean(stream, axis=-1, keepdims=True)
    centered = stream - row_mean
    variance = jnp.mean(centered * centered, axis=-1, keepdims=True)
    inverse = lax.rsqrt(variance + eps_norm)
    normed = centered * inverse
    return (normed * gain + shift, normed, inverse)


def norm_backward(upstream, normed, inverse, gain):
    scaled = upstream * gain
    row_inner = jnp.mean(scaled, axis=-1, keepdims=True)
    row_corr = jnp.mean(scaled * normed, axis=-1, keepdims=True)
    stream_grad = inverse * (scaled - row_inner - normed * row_corr)
    return (stream_grad, jnp.sum(upstream * normed, axis=0), jnp.sum(upstream, axis=0))


def gelu_pair(pre_act):
    tanh_val = jnp.tanh(gelu_coef * (pre_act + 0.044715 * pre_act * pre_act * pre_act))
    gelu_out = 0.5 * pre_act * (1.0 + tanh_val)
    gelu_slope = 0.5 * (1.0 + tanh_val) + 0.5 * pre_act * (
        1.0 - tanh_val * tanh_val
    ) * gelu_coef * (1.0 + 3.0 * 0.044715 * pre_act * pre_act)
    return (gelu_out, gelu_slope)


def dot(left, right):
    return jnp.dot(left, right, preferred_element_type=f32)


def dot_nt(left, right):
    return lax.dot_general(left, right, (((1,), (1,)), ((), ())), preferred_element_type=f32)


def dot_tn(left, right):
    return lax.dot_general(left, right, (((0,), (0,)), ((), ())), preferred_element_type=f32)


def swap(value, axis, step):
    size = lax.axis_size(axis)
    return lax.ppermute(value, axis, [(place, place ^ step) for place in range(size)])


def pick(value, index, dim=0):
    return lax.dynamic_index_in_dim(value, index, dim, keepdims=False)


def stacked_heads(block):
    lane = lax.broadcasted_iota(jnp.int32, block.shape, 1)
    zero = jnp.zeros_like(block)
    return jnp.concatenate(
        [jnp.where(lane < HEAD, block, zero), jnp.where(lane < HEAD, zero, block)], axis=0
    )


def masked_scores(places, keys, two_queries, slots, rows):
    scores = dot_nt(keys, two_queries)
    key_row = lax.broadcasted_iota(jnp.int32, (rows, 2 * rows), 0)
    query_row = lax.broadcasted_iota(jnp.int32, (rows, 2 * rows), 1)
    ahead = key_row - jnp.where(query_row < rows, query_row, query_row - rows)
    parts = []
    for slot in range(slots):
        piece = scores[slot * rows : (slot + 1) * rows]
        parts.append(jnp.where(ahead <= places[0] - places[1 + slot], piece, -1e30))
    return parts


def forward_kernel(places, q_ref, *refs):
    slots = (len(refs) - 2) // 2
    key_refs, value_refs = refs[:slots], refs[slots : 2 * slots]
    out_ref, lse_ref = refs[2 * slots :]
    rows = q_ref.shape[1]
    keys = jnp.concatenate([ref[0] for ref in key_refs], axis=0)
    values = jnp.concatenate([ref[0] for ref in value_refs], axis=0)
    two_queries = stacked_heads(q_ref[0] * 0.125)
    parts = masked_scores(places, keys, two_queries, slots, rows)
    top = jnp.max(parts[0], axis=0, keepdims=True)
    for piece in parts[1:]:
        top = jnp.maximum(top, jnp.max(piece, axis=0, keepdims=True))
    parts = [jnp.exp(piece - top) for piece in parts]
    total = jnp.sum(parts[0], axis=0, keepdims=True)
    for piece in parts[1:]:
        total = total + jnp.sum(piece, axis=0, keepdims=True)
    inverse = 1.0 / total
    probs = jnp.concatenate([(piece * inverse).astype(bf16) for piece in parts], axis=0)
    mixed = dot_tn(values, probs)
    chosen = jnp.concatenate([mixed[:HEAD, :rows], mixed[HEAD:, rows:]], axis=0)
    out_ref[0] = chosen.T.astype(bf16)
    lse_ref[0, 0] = top + jnp.log(total)


def backward_kernel(places, q_ref, grad_ref, lse_ref, *refs):
    slots = (len(refs) - 3) // 2
    key_refs, value_refs = refs[:slots], refs[slots : 2 * slots]
    dq_ref, dk_ref, dv_ref = refs[2 * slots :]
    rows = q_ref.shape[1]
    keys = jnp.concatenate([ref[0] for ref in key_refs], axis=0)
    values = jnp.concatenate([ref[0] for ref in value_refs], axis=0)
    two_queries = stacked_heads(q_ref[0] * 0.125)
    two_grads = stacked_heads(grad_ref[0])
    lse = lse_ref[0, 0]
    parts = [jnp.exp(piece - lse) for piece in masked_scores(places, keys, two_queries, slots, rows)]
    prob_grad = dot_nt(values, two_grads)
    delta = jnp.zeros_like(lse)
    for slot in range(slots):
        delta = delta + jnp.sum(
            parts[slot] * prob_grad[slot * rows : (slot + 1) * rows], axis=0, keepdims=True
        )
    score_grad = jnp.concatenate(
        [
            (parts[slot] * (prob_grad[slot * rows : (slot + 1) * rows] - delta)).astype(bf16)
            for slot in range(slots)
        ],
        axis=0,
    )
    probs = jnp.concatenate([piece.astype(bf16) for piece in parts], axis=0)
    dk_ref[:, 0] = dot(score_grad, two_queries).astype(bf16).reshape(slots, rows, 2 * HEAD)
    dv_ref[:, 0] = dot(probs, two_grads).astype(bf16).reshape(slots, rows, 2 * HEAD)
    mixed = dot_tn(keys, score_grad)
    chosen = jnp.concatenate([mixed[:HEAD, :rows], mixed[HEAD:, rows:]], axis=0) * 0.125
    dq_ref[0] = chosen.T.astype(bf16)


def column_spec(rows, first):
    return pl.BlockSpec((1, rows, 2 * HEAD), lambda s, h, places: (s, 0, first + h))


def kv_specs(rows, slots):
    pairs = HEADS // 2
    keys = [column_spec(rows, pairs)] + [column_spec(rows, 0)] * (slots - 1)
    values = [column_spec(rows, 2 * pairs)] + [column_spec(rows, pairs)] * (slots - 1)
    return keys + values


def attend(places, projected, others):
    seqs, rows, _ = projected.shape
    pairs, slots = HEADS // 2, 1 + len(others)
    lse_spec = pl.BlockSpec((1, 1, 1, 2 * rows), lambda s, h, places: (s, h, 0, 0))
    return pl.pallas_call(
        forward_kernel,
        grid_spec=pltpu.PrefetchScalarGridSpec(
            num_scalar_prefetch=1,
            grid=(seqs, pairs),
            in_specs=[column_spec(rows, 0)] + kv_specs(rows, slots),
            out_specs=[column_spec(rows, 0), lse_spec],
        ),
        out_shape=[
            jax.ShapeDtypeStruct((seqs, rows, HEADS * HEAD), bf16),
            jax.ShapeDtypeStruct((seqs, pairs, 1, 2 * rows), f32),
        ],
        compiler_params=pltpu.CompilerParams(vmem_limit_bytes=56 << 20),
    )(places, projected, projected, *others, projected, *others)


def attend_back(places, projected, others, grad_rows, lse):
    seqs, rows, _ = projected.shape
    pairs, slots = HEADS // 2, 1 + len(others)
    lse_spec = pl.BlockSpec((1, 1, 1, 2 * rows), lambda s, h, places: (s, h, 0, 0))
    slot_spec = pl.BlockSpec((slots, 1, rows, 2 * HEAD), lambda s, h, places: (0, s, 0, h))
    return pl.pallas_call(
        backward_kernel,
        grid_spec=pltpu.PrefetchScalarGridSpec(
            num_scalar_prefetch=1,
            grid=(seqs, pairs),
            in_specs=[column_spec(rows, 0), column_spec(rows, 0), lse_spec] + kv_specs(rows, slots),
            out_specs=[column_spec(rows, 0), slot_spec, slot_spec],
        ),
        out_shape=[
            jax.ShapeDtypeStruct((seqs, rows, HEADS * HEAD), bf16),
            jax.ShapeDtypeStruct((slots, seqs, rows, HEADS * HEAD), bf16),
            jax.ShapeDtypeStruct((slots, seqs, rows, HEADS * HEAD), bf16),
        ],
        compiler_params=pltpu.CompilerParams(vmem_limit_bytes=56 << 20),
    )(places, projected, grad_rows, lse, projected, *others, projected, *others)


def gather_shards(shard):
    depth, place = lax.axis_size("z"), lax.axis_index("z")
    found = jnp.stack([shard] + [swap(shard, "z", step) for step in range(1, depth)])
    line = jnp.stack([pick(found, slot ^ place) for slot in range(depth)])
    whole = lax.all_gather(line, PLANE, axis=1, tiled=True)
    return whole.reshape(-1, shard.shape[1])


def finish_over_z(line):
    depth, place = lax.axis_size("z"), lax.axis_index("z")
    total = pick(line, place).astype(f32)
    for step in range(1, depth):
        total = total + swap(pick(line, place ^ step), "z", step).astype(f32)
    return total


def scatter_sum(partial):
    depth = lax.axis_size("z")
    line = lax.psum_scatter(
        partial.reshape(depth, -1, partial.shape[1]), PLANE, scatter_dimension=1, tiled=True
    )
    return finish_over_z(line)


def plane_steps():
    tall, wide = lax.axis_size("y"), lax.axis_size("x")
    return [(core, down, along) for core in (0, 1) for down in range(tall) for along in range(wide)]


def gather_rows(own):
    tall, wide = lax.axis_size("y"), lax.axis_size("x")
    near = {(0, 0): own}
    if tall == 2 and wide == 2:
        near[0, 1] = swap(own, "x", 1)
        near[1, 0] = swap(own, "y", 1)
        near[1, 1] = jnp.concatenate([swap(near[1, 0][:1], "x", 1), swap(near[0, 1][1:], "y", 1)])
    else:
        for down in range(tall):
            for along in range(wide):
                value = swap(own, "y", down) if down else own
                near[down, along] = swap(value, "x", along) if along else value
    far = {place: swap(value, "c", 1) for place, value in near.items()}
    found = [(far if core else near)[down, along] for core, down, along in plane_steps()]
    return found[1:]


def scatter_rows(terms):
    tall, wide = lax.axis_size("y"), lax.axis_size("x")
    half = tall * wide
    chip = (terms[:half].astype(f32) + swap(terms[half:], "c", 1).astype(f32)).astype(bf16)
    chip = chip.reshape((tall, wide) + terms.shape[1:])

    def over(value, axis):
        total = value[0].astype(f32)
        for step in range(1, value.shape[0]):
            total = total + swap(value[step], axis, step).astype(f32)
        return total.astype(bf16)

    first = over(over(jnp.swapaxes(chip[:, :, :1], 0, 1), "x"), "y")
    second = over(over(chip[:, :, 1:], "y"), "x")
    return jnp.concatenate([first, second])


def scatter_sum_split(left, right):
    depth, tall, wide = lax.axis_size("z"), lax.axis_size("y"), lax.axis_size("x")
    spot_y, spot_x, spot_c = lax.axis_index("y"), lax.axis_index("x"), lax.axis_index("c")

    def over(value, axis, spot):
        dim = value.ndim - 3
        total = pick(value, spot, dim).astype(f32)
        for step in range(1, lax.axis_size(axis)):
            total = total + swap(pick(value, spot ^ step, dim), axis, step).astype(f32)
        return total.astype(bf16)

    halves = []
    for value, order in ((left, "xy"), (right, "yx")):
        value = value.reshape(depth, tall, wide, 2, -1, value.shape[1])
        value = over(value, "c", spot_c)
        if order == "xy":
            value = over(over(value, "x", spot_x), "y", spot_y)
        else:
            value = over(over(jnp.swapaxes(value, 1, 2), "y", spot_y), "x", spot_x)
        halves.append(value)
    return finish_over_z(jnp.concatenate(halves, axis=-1))


def per_device(
    patches, w_in, b_in, g_one, s_one, w_qkv, w_out, b_out, g_two, s_two, w_up, b_up, w_down, b_down,
    cotangent,
):
    seqs, rows, in_width = patches.shape
    width = w_out.shape[1]
    ff = w_up.shape[1]
    tall, wide = lax.axis_size("y"), lax.axis_size("x")
    devices = lax.axis_size("z") * tall * wide * 2
    spot = (lax.axis_index("y") * wide + lax.axis_index("x")) * 2 + lax.axis_index("c")
    steps = np.array([(down * wide + along) * 2 + core for core, down, along in plane_steps()])
    places = jnp.concatenate([spot[None], spot ^ jnp.asarray(steps, jnp.int32)]) * rows

    vectors = (b_in, g_one, s_one, b_out, g_two, s_two, b_down, b_up)
    small = b_in.shape[0]
    packed = jnp.concatenate(vectors)
    extra = jnp.zeros((8, width), bf16).at[0, : packed.shape[0]].set(packed)

    in_rows = w_in.shape[0]
    half = in_rows // 2
    first = gather_shards(jnp.concatenate([w_in[:half], extra]))
    second = gather_shards(w_in[half:])
    middle = gather_shards(jnp.concatenate([w_qkv, w_out], axis=1))
    up_all = gather_shards(w_up)
    down_all = gather_shards(w_down)
    first = first.reshape(devices, half + 8, width)
    in_all = jnp.concatenate(
        [first[:, :half], second.reshape(devices, half, width)], axis=1
    ).reshape(in_width, width)
    vec = first[:, half, : packed.shape[0]].astype(f32)
    vec_small = vec[:, : 7 * small].reshape(devices, 7, small).transpose(1, 0, 2).reshape(7, width)
    all_b_in, gain_one, shift_one, all_b_out, gain_two, shift_two, all_b_down = vec_small
    all_b_up = vec[:, 7 * small :].reshape(ff)
    qkv_all, out_all = middle[:, : 3 * width], middle[:, 3 * width :]

    flat = patches.reshape(seqs * rows, in_width)
    h_zero = dot(flat, in_all) + all_b_in
    n_one, normed_one, inverse_one = norm_forward(h_zero, gain_one, shift_one)
    a_one = n_one.astype(bf16)
    projected = dot(a_one, qkv_all).astype(bf16).reshape(seqs, rows, 3 * width)
    others = gather_rows(projected[:, :, width:])
    attended, lse = attend(places, projected, others)
    attended = attended.reshape(seqs * rows, width)
    h_one = h_zero + dot(attended, out_all) + all_b_out
    n_two, normed_two, inverse_two = norm_forward(h_one, gain_two, shift_two)
    a_two = n_two.astype(bf16)
    pre_act = dot(a_two, up_all) + all_b_up
    gelu_out, gelu_slope = gelu_pair(pre_act)
    hidden = gelu_out.astype(bf16)
    result = h_one + dot(hidden, down_all) + all_b_down
    block_out = result.astype(bf16).reshape(seqs, rows, width)

    cot = cotangent.reshape(seqs * rows, width)
    cot_float = cot.astype(f32)
    grad_b_down = jnp.sum(cot_float, axis=0)
    grad_w_down = scatter_sum(dot_tn(hidden, cot).astype(bf16))
    pre_grad = dot_nt(cot, down_all) * gelu_slope
    grad_b_up = jnp.sum(pre_grad, axis=0)
    up_grad = pre_grad.astype(bf16)
    grad_w_up = scatter_sum(dot_tn(a_two, up_grad).astype(bf16))
    two_grad = dot_nt(up_grad, up_all)
    norm_grad, grad_g_two, grad_s_two = norm_backward(two_grad, normed_two, inverse_two, gain_two)
    stream_one = cot_float + norm_grad
    grad_b_out = jnp.sum(stream_one, axis=0)
    out_grad = stream_one.astype(bf16)
    attended_grad = dot_nt(out_grad, out_all).astype(bf16).reshape(seqs, rows, width)
    dq, dk, dv = attend_back(places, projected, others, attended_grad, lse)
    dkv = scatter_rows(jnp.concatenate([dk, dv], axis=-1))
    projected_grad = jnp.concatenate([dq, dkv], axis=-1).reshape(seqs * rows, 3 * width)
    grad_middle = scatter_sum(
        jnp.concatenate(
            [
                dot_tn(a_one, projected_grad).astype(bf16),
                dot_tn(attended, out_grad).astype(bf16),
            ],
            axis=1,
        )
    )
    one_grad = dot_nt(projected_grad, qkv_all)
    norm_grad, grad_g_one, grad_s_one = norm_backward(one_grad, normed_one, inverse_one, gain_one)
    stream_zero = stream_one + norm_grad
    grad_b_in = jnp.sum(stream_zero, axis=0)
    zero_grad = stream_zero.astype(bf16)

    vec_grads = jnp.stack(
        [grad_b_in, grad_g_one, grad_s_one, grad_b_out, grad_g_two, grad_s_two, grad_b_down]
    )
    vec_grads = vec_grads.reshape(7, devices, small).transpose(1, 0, 2).reshape(devices, 7 * small)
    vec_grads = jnp.concatenate([vec_grads, grad_b_up.reshape(devices, -1)], axis=1).astype(bf16)
    tail = jnp.zeros((devices, 8, width), bf16).at[:, 0, : vec_grads.shape[1]].set(vec_grads)
    column = width // 2
    in_halves = []
    for start in (0, column):
        part = dot_tn(flat, zero_grad[:, start : start + column]).astype(bf16)
        part = part.reshape(devices, in_rows, column)
        part = jnp.concatenate([part, tail[:, :, start : start + column]], axis=1)
        in_halves.append(part.reshape(devices * (in_rows + 8), column))
    grad_in = scatter_sum_split(*in_halves)
    grad_patches = dot_nt(zero_grad, in_all).reshape(seqs, rows, in_width)

    vec_own = grad_in[in_rows]
    small_grads = [vec_own[index * small : (index + 1) * small] for index in range(7)]
    grad_b_up = vec_own[7 * small : 7 * small + b_up.shape[0]]
    return (
        block_out,
        grad_patches,
        grad_in[:in_rows],
        small_grads[0],
        small_grads[1],
        small_grads[2],
        grad_middle[:, : 3 * width],
        grad_middle[:, 3 * width :],
        small_grads[3],
        small_grads[4],
        small_grads[5],
        grad_w_up,
        grad_b_up,
        grad_w_down,
        small_grads[6],
    )


def solution(mesh):
    depth, plane = mesh.shape["dp"], mesh.shape["ctx"]
    side = math.isqrt(plane // 2)
    fine = Mesh(mesh.devices.reshape(depth, plane // 2 // side, side, 2), ALL)
    matrix, vector, rows = P(ALL, None), P(ALL), P("z", PLANE, None)
    weights = (
        matrix, vector, vector, vector, matrix, matrix, vector, vector, vector, matrix, vector,
        matrix, vector,
    )
    return jax.shard_map(
        per_device,
        mesh=fine,
        in_specs=(rows,) + weights + (rows,),
        out_specs=(rows, rows) + weights,
        check_vma=False,
    )
```

time: 1320 us -> 604 us (0.46)
  waiting for transfers between devices: 965 us -> 257 us
  blocking collectives: 83.8 us -> 0 us
  starting transfers between devices: 1.03 us -> 67.3 us
  matrix products: 124 us -> 69.6 us
  Pallas kernels: 0 us -> 32.9 us
  local copies, waits for them, and re-layouts: 91.7 us -> 117 us
  other arithmetic: 21.3 us -> 43.9 us
    reduce_scatter x4 -> x1, waiting for transfers between devices: 391 us -> 0.01 us  [scatter_sum(): lax.psum_scatter(partial.reshape(depth, -1, partial.shape[1]), PLANE, sca...]
    unnamed x17 -> x10, waiting for transfers between devices: 289 us -> 0.13 us
    all_gather x7 -> x5, waiting for transfers between devices: 285 us -> 51 us  [gather_shards(): whole = lax.all_gather(line, PLANE, axis=1, tiled=True)]
    ppermute x0 -> x46, waiting for transfers between devices: none -> 206 us  [swap(): lax.ppermute(value, axis, [(place, place ^ step) for place in range(size)])]
    unnamed x2 -> x0, blocking collectives: 83.8 us -> none
    ppermute x0 -> x46, starting transfers between devices: none -> 56.9 us  [swap(): lax.ppermute(value, axis, [(place, place ^ step) for place in range(size)])]
    dot_general x48 -> x16, matrix products: 124 us -> 69.6 us  [the longest x5 32.6 us: dot_nt(): lax.dot_general(left, right, (((1,), (1,)), ((), ())), preferred_element_...]
    pallas_call x0 -> x2, Pallas kernels: none -> 32.9 us  [the longest x1 18.7 us: attend_back(): pl.pallas_call(backward_kernel, grid_spec=pltpu.PrefetchScalarGridSpec(nu...]
  transfers between devices with their start and end apart: 14 -> 54, of which waited for: 13 -> 33; matrix products, arithmetic and copies ran while one was open for 13% -> 31% of each run, Pallas kernels for 0% -> 5%
where the time goes in v1:
time: 604 us; the launch traced here: 603 us
  waiting for transfers between devices  257 us (43%)
  local copies, waits for them, and re-layouts  117 us (19%)
  matrix products  69.6 us (12%)
  starting transfers between devices  67.3 us (11%)
  other arithmetic  43.9 us (7%)
  Pallas kernels  32.9 us (5%)
  between operations  15.3 us (3%)
    ppermute x46, waiting for transfers between devices, swap(): lax.ppermute(value, axis, [(place, place ^ step) for place in range(size)])  206 us
    ppermute x46, starting transfers between devices, swap(): lax.ppermute(value, axis, [(place, place ^ step) for place in range(size)])  56.9 us
    all_gather x5, waiting for transfers between devices, gather_shards(): whole = lax.all_gather(line, PLANE, axis=1, tiled=True)  51 us
    unnamed x135, local copies, waits for them, and re-layouts  44.7 us
    dot_general x5, matrix products, dot_nt(): lax.dot_general(left, right, (((1,), (1,)), ((), ())), preferred_element_...  32.6 us
    dot_general x6, matrix products, dot_tn(): lax.dot_general(left, right, (((0,), (0,)), ((), ())), preferred_element_...  19.4 us
    pallas_call x1, Pallas kernels, attend_back(): pl.pallas_call(backward_kernel, grid_spec=pltpu.PrefetchScalarGridSpec(nu...  18.7 us
    dot_general x5, matrix products, dot(): return jnp.dot(left, right, preferred_element_type=f32)  17.6 us
  transfers between devices with their start and end apart: 54, of which 33 were waited for; matrix products, arithmetic and copies ran while one was open for 31% of the time, Pallas kernels for 5%

profile of v1, /device:TPU:0, one launch (start us, length us, event | category | flops | bytes accessed | tf_op | source)
XLA Modules:
  0.0 602.9 jit_solution(13817604623482560724)
XLA Ops:
  7.2 5.7 concatenate.63
  15.3 4.0 collective-permute-start.1
  20.9 7.9 %collective-permute-done.1 = bf16[104,768]{1,0:T(8,128)(2,1)} collective-permute-done((bf16[104,768]{1,0:T(8,128)(2,1)}, bf16[104,768]{1,0:T(8,128)(2,1)}, u32[]{:S(2)}, u32[]{:S(2)}) %collective-permute-start.1) | collective-permute-done | bytes 159776 | tf_op jit(solution)/shard_map/ppermute | solution.py:63
  34.0 4.9 collective-permute-start.4
  40.5 6.9 %collective-permute-done.4 = bf16[96,768]{1,0:T(8,128)(2,1)S(1)} collective-permute-done((bf16[96,768]{1,0:T(8,128)(2,1)S(1)}, bf16[96,768]{1,0:T(8,128)(2,1)S(1)}, u32[]{:S(2)}, u32[]{:S(2)}) %collective-permute-start.4) | collective-permute-done | bytes 147488 | tf_op jit(solution)/shard_map/ppermute | solution.py:63
  57.0 4.1 collective-permute-done.8
  61.1 7.2 %collective-permute-done.7 = bf16[24,3072]{1,0:T(8,128)(2,1)S(1)} collective-permute-done((bf16[24,3072]{1,0:T(8,128)(2,1)S(1)}, bf16[24,3072]{1,0:T(8,128)(2,1)S(1)}, u32[]{:S(2)}, u32[]{:S(2)}) %collective-permute-start.7) | collective-permute-done | bytes 147488 | tf_op jit(solution)/shard_map/ppermute | solution.py:63
  74.6 5.6 collective-permute-done.19
  80.2 5.6 collective-permute-done.18
  90.5 3.9 collective-permute-done.20
  97.4 5.1 collective-permute-done.21
  104.9 4.9 slice.235
  110.9 7.1 %all-gather.8.cloned.1.call-done = bf16[4,768,768]{2,1,0:T(8,128)(2,1)} async-done(((bf16[4,96,768]{2,1,0:T(8,128)(2,1)}), bf16[4,768,768]{2,1,0:T(8,128)(2,1)}) %all-gather.8.cloned.1.call-update) | async-done | bytes 4718608 | tf_op jit(solution)/shard_map/all_gather | solution.py:203
  118.0 4.5 pad_maximum_fusion
  127.4 32.1 %all-gather.10.cloned.1.call-done = bf16[4,192,3072]{2,1,0:T(8,128)(2,1)} async-done(((bf16[4,24,3072]{2,1,0:T(8,128)(2,1)}), bf16[4,192,3072]{2,1,0:T(8,128)(2,1)}) %all-gather.10.cloned.1.call-update) | async-done | bytes 4718608 | tf_op jit(solution)/shard_map/all_gather | solution.py:203
  166.9 24.3 %collective-permute-done.10.refs_2_.refs_10_ = bf16[2,128,1536]{2,1,0:T(8,128)(2,1)} collective-permute-done((bf16[2,128,1536]{2,1,0:T(8,128)(2,1)}, bf16[2,128,1536]{2,1,0:T(8,128)(2,1)}, u32[]{:S(2)}, u32[]{:S(2)}) %collective-permute-start.10) | collective-permute-done | bytes 786464 | tf_op jit(solution)/shard_map/ppermute | solution.py:63
  196.1 16.1 %collective-permute-done.11 = bf16[1,128,1536]{2,1,0:T(8,128)(2,1)S(1)} collective-permute-done((bf16[1,128,1536]{2,1,0:T(8,128)(2,1)S(1)}, bf16[1,128,1536]{2,1,0:T(8,128)(2,1)S(1)}, u32[]{:S(2)}, u32[]{:S(2)}) %collective-permute-start.11) | collective-permute-done | bytes 393248 | tf_op jit(solution)/shard_map/ppermute | solution.py:63
  216.7 14.2 %shard_map.271 = (bf16[2,128,768]{2,1,0:T(8,128)(2,1)}, f32[2,6,1,256]{3,2,1,0:T(1,128)}) custom-call(s32[9]{0:T(128)} %add_multiply_fusion.places, bf16[2,128,2304]{2,1,0:T(8,128)(2,1)} %bitcast.247, bf16[2,128,2304]{2,1,0:T(8,128)(2,1)} %bitcast.248, bf16[2,128,1536]{2,1,0:T(8,128)(2,1)} %collective-permute-done.9.refs_1_.refs_9_, ...), custom_call_target="tpu_custom_call" | custom-call | tf_op jit(solution)/shard_map/pallas_call | solution.py:161
  234.6 4.1 convolution_add_fusion
  240.4 4.4 convolution_convert_fusion.2
  244.7 11.7 %all-gather.14.cloned.1.call-done = bf16[4,768,768]{2,1,0:T(8,128)(2,1)} async-done(((bf16[4,96,768]{2,1,0:T(8,128)(2,1)}), bf16[4,768,768]{2,1,0:T(8,128)(2,1)}) %all-gather.14.cloned.1.call-update) | async-done | bytes 4718608 | tf_op jit(solution)/shard_map/all_gather | solution.py:203
  256.5 8.0 %fusion.69 = (bf16[3072]{0:T(1024)(128)(2,1)}, bf16[256,3072]{1,0:T(8,128)(2,1)}) fusion(f32[256,3072]{1,0:T(8,128)} %copy-done.55, bf16[3072,768]{1,0:T(8,128)(2,1)} %bitcast.312, bf16[256,768]{1,0:T(8,128)(2,1)S(1)} %bitcast.281), kind=kOutput, calls=%fused_computation.238 | convolution fusion | flops 1223685120 | bytes 9836544 | tf_op jit(solution)/shard_map/dot_general | solution.py:54
  264.5 9.6 %reduce-scatter.12.cloned.1.call-start = ((), (), s32[]{:S(2)}) async-start(), calls=%async_computation.10 | async-start | bytes 5308416
  274.1 6.1 %multiply_reduce_fusion = (bf16[768]{0:T(1024)(128)(2,1)}, f32[256]{0:T(256)S(1)}, f32[256]{0:T(256)S(1)}, bf16[768]{0:T(1024)(128)(2,1)}, f32[256,768]{1,0:T(8,128)S(1)}) fusion(f32[256,768]{1,0:T(8,128)} %copy-done.7, f32[256]{0:T(256)} %add_rsqrt_fusion, f32[256]{0:T(256)} %copy-done.42, f32[768]{0:T(1024)S(1)} %mul.164, ...), kind=kOutput, calls=%fused_computation.82 | convolution fusion | flops 1209726976 | bytes 7874560 | tf_op jit(solution)/shard_map/dot_general | solution.py:54
  284.6 18.7 %shard_map.272 = (bf16[2,128,768]{2,1,0:T(8,128)(2,1)}, bf16[8,2,128,768]{3,2,1,0:T(8,128)(2,1)}, bf16[8,2,128,768]{3,2,1,0:T(8,128)(2,1)}) custom-call(s32[9]{0:T(128)} %add_multiply_fusion.places, bf16[2,128,2304]{2,1,0:T(8,128)(2,1)} %bitcast.250, bf16[2,128,768]{2,1,0:T(8,128)(2,1)} %bitcast.284, f32[2,6,1,256]{3,2,1,0:T(1,128)} %get-tuple-element.45.lse_ref, ...), custom_call_target="tpu_custom_call" | custom-call | tf_op jit(solution)/shard_map/pallas_call | solution.py:182
  313.4 3.7 collective-permute-done.23
  317.1 3.8 add_convert_fusion
  324.3 3.8 convolution_convert_fusion.3
  330.8 6.0 copy.64
  336.8 3.9 copy.79
  349.3 17.2 %collective-permute-done.26 = bf16[2,1,128,1536]{3,2,0,1:T(8,128)(2,1)S(1)} collective-permute-done((bf16[2,1,128,1536]{3,2,0,1:T(8,128)(2,1)S(1)}, bf16[2,1,128,1536]{3,2,0,1:T(8,128)(2,1)S(1)}, u32[]{:S(2)}, u32[]{:S(2)}) %collective-permute-start.26) | collective-permute-done | bytes 786464 | tf_op jit(solution)/shard_map/ppermute | solution.py:63
  369.6 13.2 %collective-permute-done.25 = bf16[1,128,1536]{2,1,0:T(8,128)(2,1)S(1)} collective-permute-done((bf16[1,128,1536]{2,1,0:T(8,128)(2,1)S(1)}, bf16[1,128,1536]{2,1,0:T(8,128)(2,1)S(1)}, u32[]{:S(2)}, u32[]{:S(2)}) %collective-permute-start.25) | collective-permute-done | bytes 393248 | tf_op jit(solution)/shard_map/ppermute | solution.py:63
  382.8 3.9 collective-permute-done.27
  387.0 4.4 multiply_reduce_fusion.1
  408.7 6.7 %copy.54 = bf16[6144,384]{1,0:T(8,128)(2,1)} copy(bf16[6144,384]{0,1:T(8,128)(2,1)} %fusion) | data formatting | bytes 9437184 | tf_op jit(solution)/shard_map/convert_element_type | solution.py:378
  422.4 7.0 %copy.57 = bf16[6144,384]{1,0:T(8,128)(2,1)} copy(bf16[6144,384]{0,1:T(8,128)(2,1)} %fusion.1) | data formatting | bytes 9437184 | tf_op jit(solution)/shard_map/convert_element_type | solution.py:378
  442.3 3.9 copy.78
  458.8 30.7 %collective-permute-done.29 = bf16[4,2,200,384]{3,2,1,0:T(8,128)(2,1)} collective-permute-done((bf16[4,2,200,384]{3,2,1,0:T(8,128)(2,1)}, bf16[4,2,200,384]{3,2,1,0:T(8,128)(2,1)}, u32[]{:S(2)}, u32[]{:S(2)}) %collective-permute-start.29) | collective-permute-done | bytes 1228832 | tf_op jit(solution)/shard_map/ppermute | solution.py:63
  493.9 6.0 collective-permute-done.32
  503.0 5.4 fusion.23
  514.5 4.5 collective-permute-done.30
  520.4 4.1 collective-permute-done.33
  531.3 11.5 %fusion.70 = f32[2,128,6144]{2,1,0:T(8,128)} fusion(bf16[2,128,768]{2,1,0:T(8,128)(2,1)S(1)} %bitcast.276, bf16[6144,768,1]{1,0,2:T(8,128)(2,1)} %bitcast.256), kind=kOutput, calls=%fused_computation.239 | convolution fusion | flops 2415919104 | bytes 16121856 | tf_op jit(solution)/shard_map/dot_general | solution.py:54
  547.1 6.1 %collective-permute-done.35 = bf16[200,768]{1,0:T(8,128)(2,1)} collective-permute-done((bf16[200,768]{1,0:T(8,128)(2,1)}, bf16[200,768]{1,0:T(8,128)(2,1)}, u32[]{:S(2)}, u32[]{:S(2)}) %collective-permute-start.35) | collective-permute-done | bytes 307232 | tf_op jit(solution)/shard_map/ppermute | solution.py:63
  558.5 5.1 constant_dynamic-slice_fusion.3
  563.9 6.5 %collective-permute-start.38 = (bf16[24,3072]{1,0:T(8,128)(2,1)S(1)}, bf16[24,3072]{1,0:T(8,128)(2,1)S(1)}, u32[]{:S(2)}, u32[]{:S(2)}) collective-permute-start(bf16[24,3072]{1,0:T(8,128)(2,1)S(1)} %bitcast.310), channel_id=1, source_target_pairs={{0,16},{8,24},{16,0},{24,8},{1,17},{9,25},{17,1},{25,9},{2,18},{10... | collective-permute-start | bytes 442376 | tf_op jit(solution)/shard_map/ppermute | solution.py:63
  576.0 5.4 collective-permute-done.38
  586.4 8.6 %collective-permute-done.41 = bf16[24,3072]{1,0:T(8,128)(2,1)S(1)} collective-permute-done((bf16[24,3072]{1,0:T(8,128)(2,1)S(1)}, bf16[24,3072]{1,0:T(8,128)(2,1)S(1)}, u32[]{:S(2)}, u32[]{:S(2)}) %collective-permute-start.41) | collective-permute-done | bytes 147488 | tf_op jit(solution)/shard_map/ppermute | solution.py:63
  (330 shorter events, 189.4 us)
Async XLA Ops:
  7.2 96.8 %all-gather.6.cloned.1.call-start = ((), (), s32[]{:S(2)}) async-start(), calls=%async_computation.3 | async-start | bytes 5750784 | tf_op jit(solution)/shard_map/all_gather | solution.py:203
  15.3 13.5 %collective-permute-start.1 = (bf16[104,768]{1,0:T(8,128)(2,1)}, bf16[104,768]{1,0:T(8,128)(2,1)}, u32[]{:S(2)}, u32[]{:S(2)}) collective-permute-start(bf16[104,768]{1,0:T(8,128)(2,1)} %get-tuple-element.115), channel_id=1, source_target_pairs={{0,16},{8,24},{16,0},{24,8},{1,17},{9,25},{17,1},{25,9},{2,18},{10... | collective-permute-start | bytes 479240 | tf_op jit(solution)/shard_map/ppermute | solution.py:63
  20.9 10.9 %collective-permute-start.2 = (bf16[104,768]{1,0:T(8,128)(2,1)}, bf16[104,768]{1,0:T(8,128)(2,1)}, u32[]{:S(2)}, u32[]{:S(2)}) collective-permute-start(bf16[104,768]{1,0:T(8,128)(2,1)} %get-tuple-element.115), channel_id=1, source_target_pairs={{0,24},{8,16},{16,8},{24,0},{1,25},{9,17},{17,9},{25,1},{2,26},{10... | collective-permute-start | bytes 479240 | tf_op jit(solution)/shard_map/ppermute | solution.py:63
  34.0 84.1 %all-gather.8.cloned.1.call-start = ((), (), s32[]{:S(2)}) async-start(), calls=%async_computation.4 | async-start | bytes 5308416 | tf_op jit(solution)/shard_map/all_gather | solution.py:203
  34.0 13.3 %collective-permute-start.4 = (bf16[96,768]{1,0:T(8,128)(2,1)S(1)}, bf16[96,768]{1,0:T(8,128)(2,1)S(1)}, u32[]{:S(2)}, u32[]{:S(2)}) collective-permute-start(bf16[96,768]{1,0:T(8,128)(2,1)S(1)} %copy-done.37), channel_id=1, source_target_pairs={{0,16},{8,24},{16,0},{24,8},{1,17},{9,25},{17,1},{25,9},{2,18},{10... | collective-permute-start | bytes 442376 | tf_op jit(solution)/shard_map/ppermute | solution.py:63
  39.0 11.6 %collective-permute-start.3 = (bf16[96,768]{1,0:T(8,128)(2,1)S(1)}, bf16[96,768]{1,0:T(8,128)(2,1)S(1)}, u32[]{:S(2)}, u32[]{:S(2)}) collective-permute-start(bf16[96,768]{1,0:T(8,128)(2,1)S(1)} %copy-done.37), channel_id=1, source_target_pairs={{0,8},{8,0},{16,24},{24,16},{1,9},{9,1},{17,25},{25,17},{2,10},{10... | collective-permute-start | bytes 442376 | tf_op jit(solution)/shard_map/ppermute | solution.py:63
  39.0 11.6 %collective-permute-start.5 = (bf16[96,768]{1,0:T(8,128)(2,1)S(1)}, bf16[96,768]{1,0:T(8,128)(2,1)S(1)}, u32[]{:S(2)}, u32[]{:S(2)}) collective-permute-start(bf16[96,768]{1,0:T(8,128)(2,1)S(1)} %copy-done.37), channel_id=1, source_target_pairs={{0,24},{8,16},{16,8},{24,0},{1,25},{9,17},{17,9},{25,1},{2,26},{10... | collective-permute-start | bytes 442376 | tf_op jit(solution)/shard_map/ppermute | solution.py:63
  51.6 107.9 %all-gather.10.cloned.1.call-start = ((), (), s32[]{:S(2)}) async-start(), calls=%async_computation.5 | async-start | bytes 5308416 | tf_op jit(solution)/shard_map/all_gather | solution.py:203
  55.1 13.2 %collective-permute-start.7 = (bf16[24,3072]{1,0:T(8,128)(2,1)S(1)}, bf16[24,3072]{1,0:T(8,128)(2,1)S(1)}, u32[]{:S(2)}, u32[]{:S(2)}) collective-permute-start(bf16[24,3072]{1,0:T(8,128)(2,1)S(1)} %constant_dynamic-update-slice_fusion), channel_id=1, source_target_pairs={{0,16},{8,24},{16,0},{24,8},{1,17},{9,25},{17,1},{25,9},{2,18},{10... | collective-permute-start | bytes 442376 | tf_op jit(solution)/shard_map/ppermute | solution.py:63
  56.7 11.6 %collective-permute-start.6 = (bf16[24,3072]{1,0:T(8,128)(2,1)S(1)}, bf16[24,3072]{1,0:T(8,128)(2,1)S(1)}, u32[]{:S(2)}, u32[]{:S(2)}) collective-permute-start(bf16[24,3072]{1,0:T(8,128)(2,1)S(1)} %constant_dynamic-update-slice_fusion), channel_id=1, source_target_pairs={{0,8},{8,0},{16,24},{24,16},{1,9},{9,1},{17,25},{25,17},{2,10},{10... | collective-permute-start | bytes 442376 | tf_op jit(solution)/shard_map/ppermute | solution.py:63
  69.3 165.3 %all-gather.12.cloned.1.call-start = ((), (), s32[]{:S(2)}) async-start(), calls=%async_computation.6 | async-start | bytes 5308416 | tf_op jit(solution)/shard_map/all_gather | solution.py:203
  69.5 10.7 %collective-permute-start.19 = (bf16[24,3072]{1,0:T(8,128)(2,1)S(1)}, bf16[24,3072]{1,0:T(8,128)(2,1)S(1)}, u32[]{:S(2)}, u32[]{:S(2)}) collective-permute-start(bf16[24,3072]{1,0:T(8,128)(2,1)S(1)} %copy-done.35), channel_id=1, source_target_pairs={{0,24},{8,16},{16,8},{24,0},{1,25},{9,17},{17,9},{25,1},{2,26},{10... | collective-permute-start | bytes 442376 | tf_op jit(solution)/shard_map/ppermute | solution.py:63
  72.3 13.5 %collective-permute-start.18 = (bf16[24,3072]{1,0:T(8,128)(2,1)S(1)}, bf16[24,3072]{1,0:T(8,128)(2,1)S(1)}, u32[]{:S(2)}, u32[]{:S(2)}) collective-permute-start(bf16[24,3072]{1,0:T(8,128)(2,1)S(1)} %copy-done.35), channel_id=1, source_target_pairs={{0,16},{8,24},{16,0},{24,8},{1,17},{9,25},{17,1},{25,9},{2,18},{10... | collective-permute-start | bytes 442376 | tf_op jit(solution)/shard_map/ppermute | solution.py:63
  86.9 169.6 %all-gather.14.cloned.1.call-start = ((), (), s32[]{:S(2)}) async-start(), calls=%async_computation.7 | async-start | bytes 5308416 | tf_op jit(solution)/shard_map/all_gather | solution.py:203
  87.0 10.4 %collective-permute-start.22 = (bf16[96,768]{1,0:T(8,128)(2,1)S(1)}, bf16[96,768]{1,0:T(8,128)(2,1)S(1)}, u32[]{:S(2)}, u32[]{:S(2)}) collective-permute-start(bf16[96,768]{1,0:T(8,128)(2,1)S(1)} %copy-done.36), channel_id=1, source_target_pairs={{0,24},{8,16},{16,8},{24,0},{1,25},{9,17},{17,9},{25,1},{2,26},{10... | collective-permute-start | bytes 442376 | tf_op jit(solution)/shard_map/ppermute | solution.py:63
  89.7 12.8 %collective-permute-start.21 = (bf16[96,768]{1,0:T(8,128)(2,1)S(1)}, bf16[96,768]{1,0:T(8,128)(2,1)S(1)}, u32[]{:S(2)}, u32[]{:S(2)}) collective-permute-start(bf16[96,768]{1,0:T(8,128)(2,1)S(1)} %copy-done.36), channel_id=1, source_target_pairs={{0,16},{8,24},{16,0},{24,8},{1,17},{9,25},{17,1},{25,9},{2,18},{10... | collective-permute-start | bytes 442376 | tf_op jit(solution)/shard_map/ppermute | solution.py:63
  103.5 404.9 %reduce-scatter.8.cloned.1.call-start = ((), (), s32[]{:S(2)}) async-start(), calls=%async_computation.8 | async-start | bytes 5308416 | tf_op jit(solution)/shard_map/reduce_scatter | solution.py:217
  164.9 26.3 %collective-permute-start.10 = (bf16[2,128,1536]{2,1,0:T(8,128)(2,1)}, bf16[2,128,1536]{2,1,0:T(8,128)(2,1)}, u32[]{:S(2)}, u32[]{:S(2)}) collective-permute-start(bf16[2,128,1536]{2,1,0:T(8,128)(2,1)} %slice.239), channel_id=1, source_target_pairs={{0,4},{4,0},{1,5},{5,1},{2,6},{6,2},{3,7},{7,3},{8,12},{12,8},{9,1... | collective-permute-start | bytes 2359304 | tf_op jit(solution)/shard_map/ppermute | solution.py:63
  166.2 27.6 %collective-permute-start.9 = (bf16[2,128,1536]{2,1,0:T(8,128)(2,1)}, bf16[2,128,1536]{2,1,0:T(8,128)(2,1)}, u32[]{:S(2)}, u32[]{:S(2)}) collective-permute-start(bf16[2,128,1536]{2,1,0:T(8,128)(2,1)} %slice.239), channel_id=1, source_target_pairs={{0,2},{2,0},{1,3},{3,1},{4,6},{6,4},{5,7},{7,5},{8,10},{10,8},{9,1... | collective-permute-start | bytes 2359304 | tf_op jit(solution)/shard_map/ppermute | solution.py:63
  192.3 19.9 %collective-permute-start.11 = (bf16[1,128,1536]{2,1,0:T(8,128)(2,1)S(1)}, bf16[1,128,1536]{2,1,0:T(8,128)(2,1)S(1)}, u32[]{:S(2)}, u32[]{:S(2)}) collective-permute-start(bf16[1,128,1536]{2,1,0:T(8,128)(2,1)S(1)} %slice.240), channel_id=1, source_target_pairs={{0,2},{2,0},{1,3},{3,1},{4,6},{6,4},{5,7},{7,5},{8,10},{10,8},{9,1... | collective-permute-start | bytes 1179656 | tf_op jit(solution)/shard_map/ppermute | solution.py:63
  194.9 18.4 %collective-permute-start.12 = (bf16[1,128,1536]{2,1,0:T(8,128)(2,1)S(1)}, bf16[1,128,1536]{2,1,0:T(8,128)(2,1)S(1)}, u32[]{:S(2)}, u32[]{:S(2)}) collective-permute-start(bf16[1,128,1536]{2,1,0:T(8,128)(2,1)S(1)} %slice.241), channel_id=1, source_target_pairs={{0,4},{4,0},{1,5},{5,1},{2,6},{6,2},{3,7},{7,3},{8,12},{12,8},{9,1... | collective-permute-start | bytes 1179656 | tf_op jit(solution)/shard_map/ppermute | solution.py:63
  195.6 20.1 %collective-permute-start.13 = (bf16[2,128,1536]{2,1,0:T(8,128)(2,1)}, bf16[2,128,1536]{2,1,0:T(8,128)(2,1)}, u32[]{:S(2)}, u32[]{:S(2)}) collective-permute-start(bf16[2,128,1536]{2,1,0:T(8,128)(2,1)} %slice.239), channel_id=1, source_target_pairs={{0,1},{1,0},{2,3},{3,2},{4,5},{5,4},{6,7},{7,6},{8,9},{9,8},{10,11... | collective-permute-start | bytes 2359304 | tf_op jit(solution)/shard_map/ppermute | solution.py:63
  195.6 20.1 %collective-permute-start.15 = (bf16[2,128,1536]{2,1,0:T(8,128)(2,1)}, bf16[2,128,1536]{2,1,0:T(8,128)(2,1)}, u32[]{:S(2)}, u32[]{:S(2)}) collective-permute-start(bf16[2,128,1536]{2,1,0:T(8,128)(2,1)} %collective-permute-done.10.refs_2_.refs_10_), channel_id=1, source_target_pairs={{0,1},{1,0},{2,3},{3,2},{4,5},{5,4},{6,7},{7,6},{8,9},{9,8},{10,11... | collective-permute-start | bytes 2359304 | tf_op jit(solution)/shard_map/ppermute | solution.py:63
  196.1 19.6 %collective-permute-start.14 = (bf16[2,128,1536]{2,1,0:T(8,128)(2,1)}, bf16[2,128,1536]{2,1,0:T(8,128)(2,1)}, u32[]{:S(2)}, u32[]{:S(2)}) collective-permute-start(bf16[2,128,1536]{2,1,0:T(8,128)(2,1)} %collective-permute-done.9.refs_1_.refs_9_), channel_id=1, source_target_pairs={{0,1},{1,0},{2,3},{3,2},{4,5},{5,4},{6,7},{7,6},{8,9},{9,8},{10,11... | collective-permute-start | bytes 2359304 | tf_op jit(solution)/shard_map/ppermute | solution.py:63
  264.5 278.3 %reduce-scatter.12.cloned.1.call-start = ((), (), s32[]{:S(2)}) async-start(), calls=%async_computation.10 | async-start | bytes 5308416
  322.0 25.1 %collective-permute-start.24 = (bf16[2,1,128,1536]{3,2,1,0:T(8,128)(2,1)}, bf16[2,1,128,1536]{3,2,1,0:T(8,128)(2,1)}, u32[]{:S(2)}, u32[]{:S(2)}) collective-permute-start(bf16[2,1,128,1536]{3,2,1,0:T(8,128)(2,1)} %slice_bitcast_fusion.2), channel_id=1, source_target_pairs={{0,2},{2,0},{1,3},{3,1},{4,6},{6,4},{5,7},{7,5},{8,10},{10,8},{9,1... | collective-permute-start | bytes 2359304 | tf_op jit(solution)/shard_map/ppermute | solution.py:63
  340.8 215.4 %reduce-scatter.10.cloned.1.call-start = ((), (), s32[]{:S(2)}) async-start(), calls=%async_computation.9 | async-start | bytes 5308416
  345.7 20.8 %collective-permute-start.26 = (bf16[2,1,128,1536]{3,2,0,1:T(8,128)(2,1)S(1)}, bf16[2,1,128,1536]{3,2,0,1:T(8,128)(2,1)S(1)}, u32[]{:S(2)}, u32[]{:S(2)}) collective-permute-start(bf16[2,1,128,1536]{3,2,0,1:T(8,128)(2,1)S(1)} %slice_bitcast_fusion), channel_id=1, source_target_pairs={{0,4},{4,0},{1,5},{5,1},{2,6},{6,2},{3,7},{7,3},{8,12},{12,8},{9,1... | collective-permute-start | bytes 2359304 | tf_op jit(solution)/shard_map/ppermute | solution.py:63
  348.5 34.2 %collective-permute-start.25 = (bf16[1,128,1536]{2,1,0:T(8,128)(2,1)S(1)}, bf16[1,128,1536]{2,1,0:T(8,128)(2,1)S(1)}, u32[]{:S(2)}, u32[]{:S(2)}) collective-permute-start(bf16[1,128,1536]{2,1,0:T(8,128)(2,1)S(1)} %slice_bitcast_fusion.6), channel_id=1, source_target_pairs={{0,4},{4,0},{1,5},{5,1},{2,6},{6,2},{3,7},{7,3},{8,12},{12,8},{9,1... | collective-permute-start | bytes 1179656 | tf_op jit(solution)/shard_map/ppermute | solution.py:63
  368.0 18.8 %collective-permute-start.27 = (bf16[1,128,1536]{2,1,0:T(8,128)(2,1)S(1)}, bf16[1,128,1536]{2,1,0:T(8,128)(2,1)S(1)}, u32[]{:S(2)}, u32[]{:S(2)}) collective-permute-start(bf16[1,128,1536]{2,1,0:T(8,128)(2,1)S(1)} %slice_bitcast_fusion.4), channel_id=1, source_target_pairs={{0,2},{2,0},{1,3},{3,1},{4,6},{6,4},{5,7},{7,5},{8,10},{10,8},{9,1... | collective-permute-start | bytes 1179656 | tf_op jit(solution)/shard_map/ppermute | solution.py:63
  418.8 27.5 %collective-permute-start.28 = (bf16[4,2,2,200,384]{4,3,2,1,0:T(8,128)(2,1)}, bf16[4,2,2,200,384]{4,3,2,1,0:T(8,128)(2,1)}, u32[]{:S(2)}, u32[]{:S(2)}) collective-permute-start(bf16[4,2,2,200,384]{4,3,2,1,0:T(8,128)(2,1)} %fusion.14), channel_id=1, source_target_pairs={{0,1},{1,0},{2,3},{3,2},{4,5},{5,4},{6,7},{7,6},{8,9},{9,8},{10,11... | collective-permute-start | bytes 7372808 | tf_op jit(solution)/shard_map/ppermute | solution.py:63
  436.1 14.8 %collective-permute-start.31 = (bf16[4,2,2,200,384]{4,3,0,2,1:T(8,128)(2,1)}, bf16[4,2,2,200,384]{4,3,0,2,1:T(8,128)(2,1)}, u32[]{:S(2)}, u32[]{:S(2)}) collective-permute-start(bf16[4,2,2,200,384]{4,3,0,2,1:T(8,128)(2,1)} %bitcast.236), channel_id=1, source_target_pairs={{0,1},{1,0},{2,3},{3,2},{4,5},{5,4},{6,7},{7,6},{8,9},{9,8},{10,11... | collective-permute-start | bytes 7372808 | tf_op jit(solution)/shard_map/ppermute | solution.py:63
  450.6 38.9 %collective-permute-start.29 = (bf16[4,2,200,384]{3,2,1,0:T(8,128)(2,1)}, bf16[4,2,200,384]{3,2,1,0:T(8,128)(2,1)}, u32[]{:S(2)}, u32[]{:S(2)}) collective-permute-start(bf16[4,2,200,384]{3,2,1,0:T(8,128)(2,1)} %dynamic-slice_bitcast_fusion.1), channel_id=1, source_target_pairs={{0,2},{2,0},{1,3},{3,1},{4,6},{6,4},{5,7},{7,5},{8,10},{10,8},{9,1... | collective-permute-start | bytes 3686408 | tf_op jit(solution)/shard_map/ppermute | solution.py:63
  457.0 42.8 %collective-permute-start.32 = (bf16[4,2,200,384]{3,2,0,1:T(8,128)(2,1)}, bf16[4,2,200,384]{3,2,0,1:T(8,128)(2,1)}, u32[]{:S(2)}, u32[]{:S(2)}) collective-permute-start(bf16[4,2,200,384]{3,2,0,1:T(8,128)(2,1)} %dynamic-slice_bitcast_fusion), channel_id=1, source_target_pairs={{0,4},{4,0},{1,5},{5,1},{2,6},{6,2},{3,7},{7,3},{8,12},{12,8},{9,1... | collective-permute-start | bytes 3686408 | tf_op jit(solution)/shard_map/ppermute | solution.py:63
  492.4 26.5 %collective-permute-start.30 = (bf16[4,200,384]{2,1,0:T(8,128)(2,1)}, bf16[4,200,384]{2,1,0:T(8,128)(2,1)}, u32[]{:S(2)}, u32[]{:S(2)}) collective-permute-start(bf16[4,200,384]{2,1,0:T(8,128)(2,1)} %dynamic-slice_bitcast_fusion.3), channel_id=1, source_target_pairs={{0,4},{4,0},{1,5},{5,1},{2,6},{6,2},{3,7},{7,3},{8,12},{12,8},{9,1... | collective-permute-start | bytes 1843208 | tf_op jit(solution)/shard_map/ppermute | solution.py:63
  502.7 21.8 %collective-permute-start.33 = (bf16[4,200,384]{2,1,0:T(8,128)(2,1)}, bf16[4,200,384]{2,1,0:T(8,128)(2,1)}, u32[]{:S(2)}, u32[]{:S(2)}) collective-permute-start(bf16[4,200,384]{2,1,0:T(8,128)(2,1)} %dynamic-slice_bitcast_fusion.2), channel_id=1, source_target_pairs={{0,2},{2,0},{1,3},{3,1},{4,6},{6,4},{5,7},{7,5},{8,10},{10,8},{9,1... | collective-permute-start | bytes 1843208 | tf_op jit(solution)/shard_map/ppermute | solution.py:63
  510.3 20.6 %collective-permute-start.43 = (bf16[96,768]{1,0:T(8,128)(2,1)S(1)}, bf16[96,768]{1,0:T(8,128)(2,1)}, u32[]{:S(2)}, u32[]{:S(2)}) collective-permute-start(bf16[96,768]{1,0:T(8,128)(2,1)S(1)} %get-tuple-element.84), channel_id=1, source_target_pairs={{0,8},{8,0},{16,24},{24,16},{1,9},{9,1},{17,25},{25,17},{2,10},{10... | collective-permute-start | bytes 442376 | tf_op jit(solution)/shard_map/ppermute | solution.py:63
  512.1 33.1 %collective-permute-start.45 = (bf16[96,768]{1,0:T(8,128)(2,1)}, bf16[96,768]{1,0:T(8,128)(2,1)}, u32[]{:S(2)}, u32[]{:S(2)}) collective-permute-start(bf16[96,768]{1,0:T(8,128)(2,1)} %get-tuple-element.85), channel_id=1, source_target_pairs={{0,24},{8,16},{16,8},{24,0},{1,25},{9,17},{17,9},{25,1},{2,26},{10... | collective-permute-start | bytes 442376 | tf_op jit(solution)/shard_map/ppermute | solution.py:63
  514.5 30.7 %collective-permute-start.44 = (bf16[96,768]{1,0:T(8,128)(2,1)}, bf16[96,768]{1,0:T(8,128)(2,1)}, u32[]{:S(2)}, u32[]{:S(2)}) collective-permute-start(bf16[96,768]{1,0:T(8,128)(2,1)} %get-tuple-element.86), channel_id=1, source_target_pairs={{0,16},{8,24},{16,0},{24,8},{1,17},{9,25},{17,1},{25,9},{2,18},{10... | collective-permute-start | bytes 442376 | tf_op jit(solution)/shard_map/ppermute | solution.py:63
  526.9 20.2 %collective-permute-start.34 = (bf16[200,768]{1,0:T(8,128)(2,1)}, bf16[200,768]{1,0:T(8,128)(2,1)}, u32[]{:S(2)}, u32[]{:S(2)}) collective-permute-start(bf16[200,768]{1,0:T(8,128)(2,1)} %get-tuple-element.70), channel_id=1, source_target_pairs={{0,8},{8,0},{16,24},{24,16},{1,9},{9,1},{17,25},{25,17},{2,10},{10... | collective-permute-start | bytes 921608 | tf_op jit(solution)/shard_map/ppermute | solution.py:63
  528.6 24.6 %collective-permute-start.35 = (bf16[200,768]{1,0:T(8,128)(2,1)}, bf16[200,768]{1,0:T(8,128)(2,1)}, u32[]{:S(2)}, u32[]{:S(2)}) collective-permute-start(bf16[200,768]{1,0:T(8,128)(2,1)} %get-tuple-element.71), channel_id=1, source_target_pairs={{0,16},{8,24},{16,0},{24,8},{1,17},{9,25},{17,1},{25,9},{2,18},{10... | collective-permute-start | bytes 921608 | tf_op jit(solution)/shard_map/ppermute | solution.py:63
  530.9 22.2 %collective-permute-start.36 = (bf16[200,768]{1,0:T(8,128)(2,1)}, bf16[200,768]{1,0:T(8,128)(2,1)}, u32[]{:S(2)}, u32[]{:S(2)}) collective-permute-start(bf16[200,768]{1,0:T(8,128)(2,1)} %get-tuple-element.72), channel_id=1, source_target_pairs={{0,24},{8,16},{16,8},{24,0},{1,25},{9,17},{17,9},{25,1},{2,26},{10... | collective-permute-start | bytes 921608 | tf_op jit(solution)/shard_map/ppermute | solution.py:63
  563.9 17.5 %collective-permute-start.38 = (bf16[24,3072]{1,0:T(8,128)(2,1)S(1)}, bf16[24,3072]{1,0:T(8,128)(2,1)S(1)}, u32[]{:S(2)}, u32[]{:S(2)}) collective-permute-start(bf16[24,3072]{1,0:T(8,128)(2,1)S(1)} %bitcast.310), channel_id=1, source_target_pairs={{0,16},{8,24},{16,0},{24,8},{1,17},{9,25},{17,1},{25,9},{2,18},{10... | collective-permute-start | bytes 442376 | tf_op jit(solution)/shard_map/ppermute | solution.py:63
  570.4 10.9 %collective-permute-start.37 = (bf16[24,3072]{1,0:T(8,128)(2,1)S(1)}, bf16[24,3072]{1,0:T(8,128)(2,1)S(1)}, u32[]{:S(2)}, u32[]{:S(2)}) collective-permute-start(bf16[24,3072]{1,0:T(8,128)(2,1)S(1)} %bitcast.307), channel_id=1, source_target_pairs={{0,8},{8,0},{16,24},{24,16},{1,9},{9,1},{17,25},{25,17},{2,10},{10... | collective-permute-start | bytes 442376 | tf_op jit(solution)/shard_map/ppermute | solution.py:63
  570.4 12.6 %collective-permute-start.39 = (bf16[24,3072]{1,0:T(8,128)(2,1)S(1)}, bf16[24,3072]{1,0:T(8,128)(2,1)S(1)}, u32[]{:S(2)}, u32[]{:S(2)}) collective-permute-start(bf16[24,3072]{1,0:T(8,128)(2,1)S(1)} %bitcast.305), channel_id=1, source_target_pairs={{0,24},{8,16},{16,8},{24,0},{1,25},{9,17},{17,9},{25,1},{2,26},{10... | collective-permute-start | bytes 442376 | tf_op jit(solution)/shard_map/ppermute | solution.py:63
  573.4 12.8 %collective-permute-start.42 = (bf16[24,3072]{1,0:T(8,128)(2,1)S(1)}, bf16[24,3072]{1,0:T(8,128)(2,1)S(1)}, u32[]{:S(2)}, u32[]{:S(2)}) collective-permute-start(bf16[24,3072]{1,0:T(8,128)(2,1)S(1)} %bitcast.309), channel_id=1, source_target_pairs={{0,24},{8,16},{16,8},{24,0},{1,25},{9,17},{17,9},{25,1},{2,26},{10... | collective-permute-start | bytes 442376 | tf_op jit(solution)/shard_map/ppermute | solution.py:63
  575.7 10.7 %collective-permute-start.40 = (bf16[24,3072]{1,0:T(8,128)(2,1)S(1)}, bf16[24,3072]{1,0:T(8,128)(2,1)S(1)}, u32[]{:S(2)}, u32[]{:S(2)}) collective-permute-start(bf16[24,3072]{1,0:T(8,128)(2,1)S(1)} %bitcast.308), channel_id=1, source_target_pairs={{0,8},{8,0},{16,24},{24,16},{1,9},{9,1},{17,25},{25,17},{2,10},{10... | collective-permute-start | bytes 442376 | tf_op jit(solution)/shard_map/ppermute | solution.py:63
  581.3 13.7 %collective-permute-start.41 = (bf16[24,3072]{1,0:T(8,128)(2,1)S(1)}, bf16[24,3072]{1,0:T(8,128)(2,1)S(1)}, u32[]{:S(2)}, u32[]{:S(2)}) collective-permute-start(bf16[24,3072]{1,0:T(8,128)(2,1)S(1)} %bitcast.306), channel_id=1, source_target_pairs={{0,16},{8,24},{16,0},{24,8},{1,17},{9,25},{17,1},{25,9},{2,18},{10... | collective-permute-start | bytes 442376 | tf_op jit(solution)/shard_map/ppermute | solution.py:63
  (63 other events, 690.1 us)
Sparse Core Ops, SparseCore 0:
  34.1 43.0 all-gather.5
  79.1 38.9 all-gather.7
  120.5 38.9 all-gather.9
  161.2 53.6 all-gather.11
  216.7 39.7 all-gather.13
  264.6 53.8 reduce-scatter.7
  340.9 62.1 reduce-scatter.11
  446.4 73.0 reduce-scatter.9

commit v2 on v1

--- a/solution.py
+++ b/solution.py
@@ -61,6 +61,10 @@
 def swap(value, axis, step):
     size = lax.axis_size(axis)
     return lax.ppermute(value, axis, [(place, place ^ step) for place in range(size)])
+
+
+def after(value, *others):
+    return lax.optimization_barrier((value,) + others)[0]
 
 
 def pick(value, index, dim=0):
@@ -112,9 +116,9 @@
 
 
 def backward_kernel(places, q_ref, grad_ref, lse_ref, *refs):
-    slots = (len(refs) - 3) // 2
+    slots = (len(refs) - 5) // 2
     key_refs, value_refs = refs[:slots], refs[slots : 2 * slots]
-    dq_ref, dk_ref, dv_ref = refs[2 * slots :]
+    dq_ref, dk_near, dk_far, dv_near, dv_far = refs[2 * slots :]
     rows = q_ref.shape[1]
     keys = jnp.concatenate([ref[0] for ref in key_refs], axis=0)
     values = jnp.concatenate([ref[0] for ref in value_refs], axis=0)
@@ -136,8 +140,11 @@
         axis=0,
     )
     probs = jnp.concatenate([piece.astype(bf16) for piece in parts], axis=0)
-    dk_ref[:, 0] = dot(score_grad, two_queries).astype(bf16).reshape(slots, rows, 2 * HEAD)
-    dv_ref[:, 0] = dot(probs, two_grads).astype(bf16).reshape(slots, rows, 2 * HEAD)
+    half = slots // 2
+    key_grad = dot(score_grad, two_queries).astype(bf16).reshape(slots, rows, 2 * HEAD)
+    value_grad = dot(probs, two_grads).astype(bf16).reshape(slots, rows, 2 * HEAD)
+    dk_near[:, 0], dk_far[:, 0] = key_grad[:half], key_grad[half:]
+    dv_near[:, 0], dv_far[:, 0] = value_grad[:half], value_grad[half:]
     mixed = dot_tn(keys, score_grad)
     chosen = jnp.concatenate([mixed[:HEAD, :rows], mixed[HEAD:, rows:]], axis=0) * 0.125
     dq_ref[0] = chosen.T.astype(bf16)
@@ -178,30 +185,30 @@
     seqs, rows, _ = projected.shape
     pairs, slots = HEADS // 2, 1 + len(others)
     lse_spec = pl.BlockSpec((1, 1, 1, 2 * rows), lambda s, h, places: (s, h, 0, 0))
-    slot_spec = pl.BlockSpec((slots, 1, rows, 2 * HEAD), lambda s, h, places: (0, s, 0, h))
+    half = slots // 2
+    slot_spec = pl.BlockSpec((half, 1, rows, 2 * HEAD), lambda s, h, places: (0, s, 0, h))
     return pl.pallas_call(
         backward_kernel,
         grid_spec=pltpu.PrefetchScalarGridSpec(
             num_scalar_prefetch=1,
             grid=(seqs, pairs),
             in_specs=[column_spec(rows, 0), column_spec(rows, 0), lse_spec] + kv_specs(rows, slots),
-            out_specs=[column_spec(rows, 0), slot_spec, slot_spec],
+            out_specs=[column_spec(rows, 0)] + [slot_spec] * 4,
         ),
-        out_shape=[
-            jax.ShapeDtypeStruct((seqs, rows, HEADS * HEAD), bf16),
-            jax.ShapeDtypeStruct((slots, seqs, rows, HEADS * HEAD), bf16),
-            jax.ShapeDtypeStruct((slots, seqs, rows, HEADS * HEAD), bf16),
-        ],
+        out_shape=[jax.ShapeDtypeStruct((seqs, rows, HEADS * HEAD), bf16)]
+        + [jax.ShapeDtypeStruct((half, seqs, rows, HEADS * HEAD), bf16)] * 4,
         compiler_params=pltpu.CompilerParams(vmem_limit_bytes=56 << 20),
     )(places, projected, grad_rows, lse, projected, *others, projected, *others)
 
 
-def gather_shards(shard):
+def gather_line(shard):
     depth, place = lax.axis_size("z"), lax.axis_index("z")
     found = jnp.stack([shard] + [swap(shard, "z", step) for step in range(1, depth)])
-    line = jnp.stack([pick(found, slot ^ place) for slot in range(depth)])
-    whole = lax.all_gather(line, PLANE, axis=1, tiled=True)
-    return whole.reshape(-1, shard.shape[1])
+    return jnp.stack([pick(found, slot ^ place) for slot in range(depth)])
+
+
+def gather_plane(line):
+    return lax.all_gather(line, PLANE, axis=1, tiled=True).reshape(-1, line.shape[2])
 
 
 def finish_over_z(line):
@@ -212,12 +219,11 @@
     return total
 
 
-def scatter_sum(partial):
-    depth = lax.axis_size("z")
-    line = lax.psum_scatter(
-        partial.reshape(depth, -1, partial.shape[1]), PLANE, scatter_dimension=1, tiled=True
-    )
-    return finish_over_z(line)
+def scatter_plane(partial):
+    depth, width = lax.axis_size("z"), partial.shape[2]
+    return lax.psum_scatter(
+        partial.reshape(depth, -1, width), PLANE, scatter_dimension=1, tiled=True
+    )
 
 
 def plane_steps():
@@ -242,44 +248,363 @@
     return found[1:]
 
 
-def scatter_rows(terms):
-    tall, wide = lax.axis_size("y"), lax.axis_size("x")
-    half = tall * wide
-    chip = (terms[:half].astype(f32) + swap(terms[half:], "c", 1).astype(f32)).astype(bf16)
-    chip = chip.reshape((tall, wide) + terms.shape[1:])
-
-    def over(value, axis):
-        total = value[0].astype(f32)
-        for step in range(1, value.shape[0]):
-            total = total + swap(value[step], axis, step).astype(f32)
-        return total.astype(bf16)
-
-    first = over(over(jnp.swapaxes(chip[:, :, :1], 0, 1), "x"), "y")
-    second = over(over(chip[:, :, 1:], "y"), "x")
-    return jnp.concatenate([first, second])
-
-
-def scatter_sum_split(left, right):
-    depth, tall, wide = lax.axis_size("z"), lax.axis_size("y"), lax.axis_size("x")
-    spot_y, spot_x, spot_c = lax.axis_index("y"), lax.axis_index("x"), lax.axis_index("c")
-
-    def over(value, axis, spot):
-        dim = value.ndim - 3
-        total = pick(value, spot, dim).astype(f32)
-        for step in range(1, lax.axis_size(axis)):
-            total = total + swap(pick(value, spot ^ step, dim), axis, step).astype(f32)
-        return total.astype(bf16)
-
-    halves = []
-    for value, order in ((left, "xy"), (right, "yx")):
-        value = value.reshape(depth, tall, wide, 2, -1, value.shape[1])
-        value = over(value, "c", spot_c)
-        if order == "xy":
-            value = over(over(value, "x", spot_x), "y", spot_y)
-        else:
-            value = over(over(jnp.swapaxes(value, 1, 2), "y", spot_y), "x", spot_x)
-        halves.append(value)
-    return finish_over_z(jnp.concatenate(halves, axis=-1))
+def add(*terms):
+    total = terms[0].astype(f32)
+    for term in terms[1:]:
+        total = total + term.astype(f32)
+    return total
+
+
+def reduce_near(terms, order):
+    def take(value, step, axis):
+        return value[step] if axis == "y" or value.ndim < terms[0].ndim else value[:, step]
+
+    inner = [take(value, 0, order[0]) for value in terms]
+    for step in range(1, lax.axis_size(order[0])):
+        send = add(*[take(value, step, order[0]) for value in terms]).astype(bf16)
+        inner.append(swap(send, order[0], step))
+    last = [value[0] for value in inner]
+    for step in range(1, lax.axis_size(order[1])):
+        send = add(*[value[step] for value in inner]).astype(bf16)
+        last.append(swap(send, order[1], step))
+    return add(*last)
+
+
+def scatter_rows(near, far, order):
+    shape = (lax.axis_size("y"), lax.axis_size("x")) + near.shape[1:]
+    return reduce_near([near.reshape(shape), swap(far, "c", 1).reshape(shape)], order).astype(bf16)
+
+
+def z_line(chunk):
+    return jnp.stack([chunk] + [swap(chunk, "z", step) for step in range(1, lax.axis_size("z"))])
+
+
+def gather_weights(shard, middle, ff, turned):
+    line = z_line(shard)
+    middle_line = gather_line(after(middle, line))
+    along, down = swap(line, "x", 1), swap(line, "y", 1)
+    far = [swap(line, "c", 1)]
+    along, down = after((along, down), middle_line, turned, *far)
+    half = (shard.shape[0] - 8) // 2
+    across = [swap(down[:, :half], "x", 1), swap(along[:, half:], "y", 1)]
+    far += [swap(along, "c", 1), swap(down, "c", 1)]
+    ff_line = gather_line(after(ff, along, down, *across))
+    far += [swap(value, "c", 1) for value in across]
+    return [line, along, down, *across, *far], after(middle_line, along, down), ff_line
+
+
+def chip_table():
+    depth = lax.axis_size("z")
+    own = (lax.axis_index("z") * 2 + lax.axis_index("y")) * 2 + lax.axis_index("x")
+    steps = jnp.arange(depth * 4, dtype=jnp.int32)
+    return jnp.concatenate([steps ^ own, lax.axis_index("c")[None]]).astype(jnp.int32)
+
+
+def pack_kernel(*refs):
+    weight, out_ref = refs[0], refs[-1]
+    rows = weight.shape[0]
+    out_ref[:rows] = weight[...]
+    out_ref[rows:] = jnp.zeros((out_ref.shape[0] - rows, out_ref.shape[1]), out_ref.dtype)
+    for place, ref in enumerate(refs[1:-1]):
+        out_ref[rows + place : rows + place + 1, : ref.shape[1]] = ref[...]
+
+
+def pack(weight, vectors):
+    return pl.pallas_call(
+        pack_kernel,
+        out_shape=jax.ShapeDtypeStruct((weight.shape[0] + 8, weight.shape[1]), weight.dtype),
+        name="pack",
+    )(weight, *[vector[None] for vector in vectors])
+
+
+def piece_specs(pieces):
+    return [pl.BlockSpec((1,) + value.shape[1:], lambda d, table: (d, 0, 0)) for value in pieces]
+
+
+def chip_weight(refs, chip, rows, core):
+    def shard(side):
+        if chip < 3:
+            return side[chip][0, :rows]
+        return jnp.concatenate([side[3][0], side[4][0, : rows // 2]], axis=0)
+
+    near, far = shard(refs[:5]), shard(refs[5:10])
+    first = jnp.where(core == 0, near, far)
+    second = jnp.where(core == 0, far, near)
+    return jnp.concatenate([first, second], axis=0)
+
+
+def chip_lanes(table, chip, lanes):
+    place = table[pl.program_id(0) * 4 + chip]
+    return pl.ds(pl.multiple_of((place % 4) * lanes, 128), lanes)
+
+
+def enter_kernel(rows, cells, table, flat_ref, *refs):
+    out_ref = refs[-1]
+
+    @pl.when(pl.program_id(0) == 0)
+    def _():
+        out_ref[...] = jnp.zeros_like(out_ref)
+
+    total = out_ref[...]
+    for chip in range(4):
+        left = flat_ref[:, chip_lanes(table, chip, 2 * rows)]
+        total = total + dot(left, chip_weight(refs, chip, rows, table[cells]))
+    out_ref[...] = total
+
+
+def leave_kernel(rows, cells, table, grad_ref, *refs):
+    out_ref = refs[-1]
+    for chip in range(4):
+        right = chip_weight(refs, chip, rows, table[cells])
+        out_ref[:, chip_lanes(table, chip, 2 * rows)] = dot_nt(grad_ref[...], right)
+
+
+def enter(table, flat, pieces, rows):
+    depth, width = lax.axis_size("z"), pieces[0].shape[2]
+    tokens, lanes = flat.shape[0], 8 * rows
+    return pl.pallas_call(
+        lambda *refs: enter_kernel(rows, depth * 4, *refs),
+        grid_spec=pltpu.PrefetchScalarGridSpec(
+            num_scalar_prefetch=1,
+            grid=(depth,),
+            in_specs=[pl.BlockSpec((tokens, lanes), lambda d, table: (0, table[d * 4] // 4))]
+            + piece_specs(pieces),
+            out_specs=pl.BlockSpec((tokens, width), lambda d, table: (0, 0)),
+        ),
+        out_shape=jax.ShapeDtypeStruct((tokens, width), f32),
+        compiler_params=pltpu.CompilerParams(vmem_limit_bytes=56 << 20),
+        name="enter",
+    )(table, flat, *pieces)
+
+
+def leave(table, grad, pieces, rows):
+    depth, width = lax.axis_size("z"), grad.shape[1]
+    tokens, lanes = grad.shape[0], 8 * rows
+    return pl.pallas_call(
+        lambda *refs: leave_kernel(rows, depth * 4, *refs),
+        grid_spec=pltpu.PrefetchScalarGridSpec(
+            num_scalar_prefetch=1,
+            grid=(depth,),
+            in_specs=[pl.BlockSpec((tokens, width), lambda d, table: (0, 0))] + piece_specs(pieces),
+            out_specs=pl.BlockSpec((tokens, lanes), lambda d, table: (0, table[d * 4] // 4)),
+        ),
+        out_shape=jax.ShapeDtypeStruct((tokens, depth * lanes), f32),
+        compiler_params=pltpu.CompilerParams(vmem_limit_bytes=56 << 20),
+        name="leave",
+    )(table, grad, *pieces)
+
+
+def turn_pair(flat, chips):
+    core = lax.axis_index("c")
+    turned = flat.T.reshape(chips, 2, -1, flat.shape[0])
+    got = swap(pick(turned, 1 - core, 1), "c", 1)
+    return jnp.concatenate([pick(turned, core, 1), got], axis=-1)
+
+
+def weight_kernel(plans, table, turned_ref, grad_ref, *out_refs):
+    columns = out_refs[0].shape[3]
+    for half, (chips, out_ref) in enumerate(zip(plans, out_refs)):
+        for place, chip in enumerate(chips):
+            left = turned_ref[table[pl.program_id(0) * 4 + chip] % 4]
+            right = grad_ref[:, half * columns : (half + 1) * columns]
+            out_ref[place, 0] = dot(left, right).astype(bf16)
+
+
+def weight_terms(table, turned, grad, plans):
+    depth = lax.axis_size("z")
+    tokens, columns = grad.shape[0], grad.shape[1] // 2
+    rows = turned.shape[1]
+    return pl.pallas_call(
+        lambda *refs: weight_kernel(plans, *refs),
+        grid_spec=pltpu.PrefetchScalarGridSpec(
+            num_scalar_prefetch=1,
+            grid=(depth,),
+            in_specs=[
+                pl.BlockSpec((4, rows, tokens), lambda d, table: (table[d * 4] // 4, 0, 0)),
+                pl.BlockSpec(grad.shape, lambda d, table: (0, 0)),
+            ],
+            out_specs=[pl.BlockSpec((2, 1, rows, columns), lambda d, table: (0, d, 0, 0))] * 2,
+        ),
+        out_shape=[jax.ShapeDtypeStruct((2, depth, rows, columns), bf16)] * 2,
+        compiler_params=pltpu.CompilerParams(vmem_limit_bytes=56 << 20),
+        name="weight_terms",
+    )(table, turned, grad)
+
+
+ORDERS = ("xy", "yx")
+
+
+def send_terms(table, turned, grad):
+    grad = jnp.concatenate([grad, swap(grad, "c", 1)], axis=0)
+    sent = weight_terms(table, turned, grad, ((1, 3), (2, 3)))
+    return grad, sent, [swap(value, order[0], 1) for value, order in zip(sent, ORDERS)]
+
+
+def finish_terms(keep, got):
+    last = [
+        swap(add(kept[1], value[1]).astype(bf16), order[1], 1)
+        for kept, value, order in zip(keep, got, ORDERS)
+    ]
+    line = [add(kept[0], value[0], other) for kept, value, other in zip(keep, got, last)]
+    line = jnp.concatenate(line, axis=-1)
+    total = line[0]
+    for step in range(1, lax.axis_size("z")):
+        total = total + swap(line[step].astype(bf16), "z", step).astype(f32)
+    return total
+
+
+def ff_kernel(a_ref, cot_ref, h_ref, b_up_ref, b_down_ref, down_ref, up_ref, *refs):
+    out_ref, two_ref, b_grad_ref, terms_ref = refs[:4]
+    total, turned, down_terms, up_terms, sems = refs[4:]
+    step, last = pl.program_id(0), pl.num_programs(0) - 1
+    width = a_ref.shape[1]
+    down_rows, up_rows = down_ref.shape[1], up_ref.shape[1]
+
+    @pl.when(step == 0)
+    def _():
+        total[...] = h_ref[...] + b_down_ref[...]
+        two_ref[...] = jnp.zeros_like(two_ref)
+        turned[...] = a_ref[...].T
+
+    up, down = up_ref[...].reshape(width, width), down_ref[...].reshape(width, width)
+    gelu_out, gelu_slope = gelu_pair(dot(a_ref[...], up) + b_up_ref[0])
+    hidden = gelu_out.astype(bf16)
+    total[...] += dot(hidden, down)
+    pre_grad = dot_nt(cot_ref[...], down) * gelu_slope
+    b_grad_ref[0] = jnp.sum(pre_grad, axis=0, keepdims=True)
+    up_grad = pre_grad.astype(bf16)
+    two_ref[...] += dot_nt(up_grad, up)
+    down_terms[step] = dot_tn(hidden, cot_ref[...]).astype(bf16).reshape(down_ref.shape)
+    up_terms[step] = dot(turned[...], up_grad).astype(bf16).reshape(up_ref.shape)
+
+    def copies(place):
+        devices = down_ref.shape[0]
+        start = down_rows + place * up_rows
+        return (
+            pltpu.make_async_copy(
+                down_terms.at[place],
+                terms_ref.at[pl.ds(place * devices, devices), pl.ds(0, down_rows)],
+                sems.at[0, place],
+            ),
+            pltpu.make_async_copy(
+                up_terms.at[place], terms_ref.at[:, pl.ds(start, up_rows)], sems.at[1, place]
+            ),
+        )
+
+    for place in range(4):
+
+        @pl.when(step == place)
+        def _():
+            for copy in copies(place):
+                copy.start()
+
+    @pl.when(step == last)
+    def _():
+        out_ref[...] = total[...].astype(bf16)
+        for place in range(4):
+            for copy in copies(place):
+                copy.wait()
+
+
+def feed_forward(a_two, cot, h_one, b_up, b_down, gathered):
+    tokens, width = a_two.shape
+    devices, rows, _ = gathered.shape
+    steps = 4
+    down_rows, up_rows = rows // 2, rows // 2 // steps
+    whole = pl.BlockSpec((tokens, width), lambda step: (0, 0))
+    line = pl.BlockSpec((1, 1, width), lambda step: (step, 0, 0))
+    down_shape, up_shape = (devices // steps, down_rows, width), (devices, up_rows, width)
+    return pl.pallas_call(
+        ff_kernel,
+        grid=(steps,),
+        in_specs=[
+            whole,
+            whole,
+            whole,
+            line,
+            pl.BlockSpec((1, width), lambda step: (0, 0)),
+            pl.BlockSpec(down_shape, lambda step: (step, 0, 0)),
+            pl.BlockSpec(up_shape, lambda step: (0, steps + step, 0)),
+        ],
+        out_specs=[whole, whole, line, pl.BlockSpec(memory_space=pl.ANY)],
+        out_shape=[
+            jax.ShapeDtypeStruct((tokens, width), bf16),
+            jax.ShapeDtypeStruct((tokens, width), f32),
+            jax.ShapeDtypeStruct((steps, 1, width), f32),
+            jax.ShapeDtypeStruct(gathered.shape, bf16),
+        ],
+        scratch_shapes=[
+            pltpu.VMEM((tokens, width), f32),
+            pltpu.VMEM((width, tokens), bf16),
+            pltpu.VMEM((steps,) + down_shape, bf16),
+            pltpu.VMEM((steps,) + up_shape, bf16),
+            pltpu.SemaphoreType.DMA((2, steps)),
+        ],
+        compiler_params=pltpu.CompilerParams(vmem_limit_bytes=56 << 20),
+        name="feed_forward",
+    )(a_two, cot, h_one, b_up.reshape(steps, 1, width), b_down[None], gathered, gathered)
+
+
+def terms_kernel(blocks, width, *refs):
+    count = len(blocks)
+    pairs, tail, out_ref = refs[: 2 * count], refs[2 * count : -1 - count], refs[-1 - count]
+    turned = refs[-count:]
+    step, group = pl.program_id(0), out_ref.shape[0]
+
+    @pl.when(step == 0)
+    def _():
+        for left, ref in zip(pairs[::2], turned):
+            ref[...] = left[...].T
+
+    start = 0
+    for index, block in enumerate(blocks):
+        rows = block[0] * group
+        left = turned[index][pl.ds(pl.multiple_of(step * rows, 16), rows), :]
+        result = dot(left, pairs[2 * index + 1][...]).astype(bf16)
+        for place in range(group):
+            for column in range(block[1]):
+                part = result[place * block[0] : (place + 1) * block[0]]
+                out_ref[place, start + column * block[0] : start + (column + 1) * block[0], :] = part[
+                    :, column * width : (column + 1) * width
+                ]
+        start += block[0] * block[1]
+    if tail:
+        out_ref[:, start:, :] = tail[0][...]
+
+
+def device_terms(pairs, devices, width, tail=None):
+    blocks = [(left.shape[1] // devices, right.shape[1] // width) for left, right in pairs]
+    rows = sum(row * block for row, block in blocks) + (0 if tail is None else tail.shape[1])
+    steps = 8
+    if devices % steps or any(row * (devices // steps) % 16 or row % 8 for row, _ in blocks):
+        parts = [by_columns(dot_tn(left, right).astype(bf16), devices, width) for left, right in pairs]
+        return jnp.concatenate(parts + ([] if tail is None else [tail]), axis=1)
+    group = devices // steps
+    operands = [value for pair in pairs for value in pair]
+    in_specs = [pl.BlockSpec(value.shape, lambda step: (0, 0)) for value in operands]
+    if tail is not None:
+        operands.append(tail)
+        in_specs.append(pl.BlockSpec((group,) + tail.shape[1:], lambda step: (step, 0, 0)))
+    return pl.pallas_call(
+        lambda *refs: terms_kernel(blocks, width, *refs),
+        grid=(steps,),
+        in_specs=in_specs,
+        out_specs=pl.BlockSpec((group, rows, width), lambda step: (step, 0, 0)),
+        out_shape=jax.ShapeDtypeStruct((devices, rows, width), bf16),
+        scratch_shapes=[pltpu.VMEM(left.shape[::-1], bf16) for left, _ in pairs],
+        compiler_params=pltpu.CompilerParams(vmem_limit_bytes=56 << 20),
+        name="device_terms",
+    )(*operands)
+
+
+def by_columns(value, devices, width):
+    value = value.reshape(devices, -1, value.shape[1] // width, width)
+    return jnp.swapaxes(value, 1, 2).reshape(devices, -1, width)
+
+
+def from_columns(value, columns):
+    blocks, width = columns // value.shape[1], value.shape[1]
+    return jnp.swapaxes(value.reshape(blocks, -1, width), 0, 1).reshape(-1, columns)
 
 
 def per_device(
@@ -296,29 +621,50 @@
     places = jnp.concatenate([spot[None], spot ^ jnp.asarray(steps, jnp.int32)]) * rows
 
     vectors = (b_in, g_one, s_one, b_out, g_two, s_two, b_down, b_up)
-    small = b_in.shape[0]
-    packed = jnp.concatenate(vectors)
-    extra = jnp.zeros((8, width), bf16).at[0, : packed.shape[0]].set(packed)
+    small, count = b_in.shape[0], b_up.shape[0]
 
     in_rows = w_in.shape[0]
     half = in_rows // 2
-    first = gather_shards(jnp.concatenate([w_in[:half], extra]))
-    second = gather_shards(w_in[half:])
-    middle = gather_shards(jnp.concatenate([w_qkv, w_out], axis=1))
-    up_all = gather_shards(w_up)
-    down_all = gather_shards(w_down)
-    first = first.reshape(devices, half + 8, width)
-    in_all = jnp.concatenate(
-        [first[:, :half], second.reshape(devices, half, width)], axis=1
-    ).reshape(in_width, width)
-    vec = first[:, half, : packed.shape[0]].astype(f32)
-    vec_small = vec[:, : 7 * small].reshape(devices, 7, small).transpose(1, 0, 2).reshape(7, width)
+    flat = patches.reshape(seqs * rows, in_width)
+    fast = tall == 2 and wide == 2 and (2 * in_rows) % 128 == 0 and half % 16 == 0
+    if fast:
+        turned = turn_pair(flat, devices // 2)
+        middle = jnp.concatenate([w_qkv, w_out], axis=1)
+        up_rows = jnp.concatenate([w_up[:, i * width : (i + 1) * width] for i in range(ff // width)])
+        pieces, middle, ff_all = gather_weights(
+            pack(w_in, vectors), middle, jnp.concatenate([w_down, up_rows]), turned
+        )
+        table = chip_table()
+        bases = [in_rows, in_rows, in_rows, None, half] * 2
+        found = [value[:, base:, :count] for value, base in zip(pieces, bases) if base is not None]
+        found = jnp.stack(found).reshape(2, 4, -1, 8 * count).transpose(2, 1, 0, 3).reshape(devices, 8 * count)
+        own = (lax.axis_index("z") * tall * wide * 2) + spot
+        order = jnp.arange(devices)[:, None] ^ own
+        chosen = (order == jnp.arange(devices)[None, :]).astype(f32)
+        vec = jnp.dot(chosen, found.astype(f32), precision=lax.Precision.HIGHEST)
+        vec = vec.reshape(devices, 8, count)
+        h_zero = enter(table, flat, pieces, in_rows)
+    else:
+        extra = jnp.stack([jnp.pad(vector, (0, width - vector.shape[0])) for vector in vectors])
+        first = gather_plane(gather_line(w_in[:half])).reshape(devices, half, width)
+        second = gather_plane(gather_line(jnp.concatenate([w_in[half:], extra])))
+        second = second.reshape(devices, half + 8, width)
+        in_all = jnp.concatenate([first, second[:, :half]], axis=1).reshape(in_width, width)
+        vec = second[:, half:, :count].astype(f32)
+        h_zero = dot(flat, in_all)
+        middle = gather_line(jnp.concatenate([w_qkv, w_out], axis=1))
+    middle = gather_plane(middle)
+    if fast:
+        ff_all = gather_plane(after(ff_all, h_zero)).reshape(devices, -1, width)
+    else:
+        up_all = gather_plane(gather_line(w_up))
+        down_all = gather_plane(gather_line(w_down))
+    vec_small = vec[:, :7, :small].transpose(1, 0, 2).reshape(7, width)
     all_b_in, gain_one, shift_one, all_b_out, gain_two, shift_two, all_b_down = vec_small
-    all_b_up = vec[:, 7 * small :].reshape(ff)
+    all_b_up = vec[:, 7].reshape(ff)
     qkv_all, out_all = middle[:, : 3 * width], middle[:, 3 * width :]
 
-    flat = patches.reshape(seqs * rows, in_width)
-    h_zero = dot(flat, in_all) + all_b_in
+    h_zero = h_zero + all_b_in
     n_one, normed_one, inverse_one = norm_forward(h_zero, gain_one, shift_one)
     a_one = n_one.astype(bf16)
     projected = dot(a_one, qkv_all).astype(bf16).reshape(seqs, rows, 3 * width)
@@ -328,38 +674,38 @@
     h_one = h_zero + dot(attended, out_all) + all_b_out
     n_two, normed_two, inverse_two = norm_forward(h_one, gain_two, shift_two)
     a_two = n_two.astype(bf16)
-    pre_act = dot(a_two, up_all) + all_b_up
-    gelu_out, gelu_slope = gelu_pair(pre_act)
-    hidden = gelu_out.astype(bf16)
-    result = h_one + dot(hidden, down_all) + all_b_down
-    block_out = result.astype(bf16).reshape(seqs, rows, width)
-
     cot = cotangent.reshape(seqs * rows, width)
     cot_float = cot.astype(f32)
     grad_b_down = jnp.sum(cot_float, axis=0)
-    grad_w_down = scatter_sum(dot_tn(hidden, cot).astype(bf16))
-    pre_grad = dot_nt(cot, down_all) * gelu_slope
-    grad_b_up = jnp.sum(pre_grad, axis=0)
-    up_grad = pre_grad.astype(bf16)
-    grad_w_up = scatter_sum(dot_tn(a_two, up_grad).astype(bf16))
-    two_grad = dot_nt(up_grad, up_all)
+    if fast:
+        result, two_grad, grad_b_up, ff_terms = feed_forward(
+            a_two, cot, h_one, all_b_up, all_b_down, ff_all
+        )
+        grad_b_up = grad_b_up.reshape(ff)
+    else:
+        pre_act = dot(a_two, up_all) + all_b_up
+        gelu_out, gelu_slope = gelu_pair(pre_act)
+        hidden = gelu_out.astype(bf16)
+        result = (h_one + dot(hidden, down_all) + all_b_down).astype(bf16)
+        pre_grad = dot_nt(cot, down_all) * gelu_slope
+        grad_b_up = jnp.sum(pre_grad, axis=0)
+        up_grad = pre_grad.astype(bf16)
+        two_grad = dot_nt(up_grad, up_all)
+        ff_terms = device_terms([(hidden, cot), (a_two, up_grad)], devices, width)
+    block_out = result.reshape(seqs, rows, width)
+    ff_sums = scatter_plane(ff_terms)
+    down_rows = w_down.shape[0]
     norm_grad, grad_g_two, grad_s_two = norm_backward(two_grad, normed_two, inverse_two, gain_two)
     stream_one = cot_float + norm_grad
     grad_b_out = jnp.sum(stream_one, axis=0)
     out_grad = stream_one.astype(bf16)
     attended_grad = dot_nt(out_grad, out_all).astype(bf16).reshape(seqs, rows, width)
-    dq, dk, dv = attend_back(places, projected, others, attended_grad, lse)
-    dkv = scatter_rows(jnp.concatenate([dk, dv], axis=-1))
-    projected_grad = jnp.concatenate([dq, dkv], axis=-1).reshape(seqs * rows, 3 * width)
-    grad_middle = scatter_sum(
-        jnp.concatenate(
-            [
-                dot_tn(a_one, projected_grad).astype(bf16),
-                dot_tn(attended, out_grad).astype(bf16),
-            ],
-            axis=1,
-        )
-    )
+    dq, dk_near, dk_far, dv_near, dv_far = attend_back(
+        places, projected, others, attended_grad, lse
+    )
+    dk = scatter_rows(dk_near, dk_far, "xy")
+    dv = scatter_rows(dv_near, dv_far, "yx")
+    projected_grad = jnp.concatenate([dq, dk, dv], axis=-1).reshape(seqs * rows, 3 * width)
     one_grad = dot_nt(projected_grad, qkv_all)
     norm_grad, grad_g_one, grad_s_one = norm_backward(one_grad, normed_one, inverse_one, gain_one)
     stream_zero = stream_one + norm_grad
@@ -369,31 +715,46 @@
     vec_grads = jnp.stack(
         [grad_b_in, grad_g_one, grad_s_one, grad_b_out, grad_g_two, grad_s_two, grad_b_down]
     )
-    vec_grads = vec_grads.reshape(7, devices, small).transpose(1, 0, 2).reshape(devices, 7 * small)
-    vec_grads = jnp.concatenate([vec_grads, grad_b_up.reshape(devices, -1)], axis=1).astype(bf16)
-    tail = jnp.zeros((devices, 8, width), bf16).at[:, 0, : vec_grads.shape[1]].set(vec_grads)
-    column = width // 2
-    in_halves = []
-    for start in (0, column):
-        part = dot_tn(flat, zero_grad[:, start : start + column]).astype(bf16)
-        part = part.reshape(devices, in_rows, column)
-        part = jnp.concatenate([part, tail[:, :, start : start + column]], axis=1)
-        in_halves.append(part.reshape(devices * (in_rows + 8), column))
-    grad_in = scatter_sum_split(*in_halves)
-    grad_patches = dot_nt(zero_grad, in_all).reshape(seqs, rows, in_width)
-
-    vec_own = grad_in[in_rows]
-    small_grads = [vec_own[index * small : (index + 1) * small] for index in range(7)]
-    grad_b_up = vec_own[7 * small : 7 * small + b_up.shape[0]]
+    vec_grads = vec_grads.reshape(7, devices, small).transpose(1, 0, 2)
+    tail = jnp.zeros((devices, 16, width), bf16).at[:, :7, :small].set(vec_grads.astype(bf16))
+    tail = tail.at[:, 7, :count].set(grad_b_up.reshape(devices, count).astype(bf16))
+    sent = []
+    if fast:
+        pair_grad, sent, got = send_terms(table, turned, zero_grad)
+        keep = weight_terms(table, turned, after(pair_grad, *sent), ((0, 2), (0, 1)))
+        sent = list(keep)
+    a_later = after(a_one, ff_sums, *sent)
+    middle_terms = device_terms(
+        [(a_later, projected_grad), (attended, out_grad)], devices, width, tail
+    )
+    grad_ff = finish_over_z(ff_sums)
+    grad_w_down, grad_w_up = grad_ff[:down_rows], from_columns(grad_ff[down_rows:], ff)
+    if fast:
+        grad_patches = leave(table, after(zero_grad, middle_terms), pieces, in_rows)
+        got = after(tuple(got), grad_patches, grad_ff)
+        grad_in = finish_terms(keep, got)
+    else:
+        grad_in = dot_tn(flat, zero_grad).astype(bf16).reshape(devices, -1, width)
+        grad_in = finish_over_z(scatter_plane(grad_in))
+        grad_patches = dot_nt(zero_grad, in_all)
+    grad_patches = grad_patches.reshape(seqs, rows, in_width)
+    grad_middle = finish_over_z(scatter_plane(middle_terms))
+    out_rows = w_out.shape[0]
+    grad_w_qkv = from_columns(grad_middle[: 3 * out_rows], 3 * width)
+    grad_w_out = grad_middle[3 * out_rows : 4 * out_rows]
+    vec_own = grad_middle[4 * out_rows :]
+
+    small_grads = vec_own[:7, :small]
+    grad_b_up = vec_own[7, :count]
     return (
         block_out,
         grad_patches,
-        grad_in[:in_rows],
+        grad_in,
         small_grads[0],
         small_grads[1],
         small_grads[2],
-        grad_middle[:, : 3 * width],
-        grad_middle[:, 3 * width :],
+        grad_w_qkv,
+        grad_w_out,
         small_grads[3],
         small_grads[4],
         small_grads[5],

time: 604 us -> 451 us (0.75)
  local copies, waits for them, and re-layouts: 117 us -> 26.2 us
  matrix products: 69.6 us -> 12.3 us
  Pallas kernels: 32.9 us -> 88.7 us
  waiting for transfers between devices: 257 us -> 221 us
  other arithmetic: 43.9 us -> 20.1 us
    pallas_call x0 -> x7, Pallas kernels: none -> 55.5 us  [the longest x1 14.2 us: feed_forward(): pl.pallas_call(ff_kernel, grid=(steps,), in_specs=[whole, whole, whole, l...]
    all_gather x5 -> x2, waiting for transfers between devices: 51 us -> 0.02 us  [gather_plane(): lax.all_gather(line, PLANE, axis=1, tiled=True).reshape(-1, line.shape[2])]
    unnamed x135 -> x79, local copies, waits for them, and re-layouts: 44.7 us -> 9.66 us
    dot_general x5 -> x2, matrix products: 32.6 us -> 6.41 us  [dot_nt(): lax.dot_general(left, right, (((1,), (1,)), ((), ())), preferred_element_...]
    dot_general x6 -> x1, matrix products: 19.4 us -> 0.2 us  [per_device(): vec = jnp.dot(chosen, found.astype(f32), precision=lax.Precision.HIGHEST)]
    convert_element_type x12, other arithmetic: 18.5 us -> 3.73 us  [the longest x2 1.5 us: reduce_near(): send = add(*[take(value, step, order[0]) for value in terms]).astype(bf16)]
    convert_element_type x2, local copies, waits for them, and re-layouts: 13.7 us -> 0.15 us  [the longest x1 0.09 us: per_device(): grad_b_up.reshape(devices, count).astype(bf16)]
    dot_general x5 -> x2, matrix products: 17.6 us -> 5.66 us  [dot(): return jnp.dot(left, right, preferred_element_type=f32)]
  transfers between devices with their start and end apart: 54 -> 51, of which waited for: 33 -> 25; matrix products, arithmetic and copies ran while one was open for 31% -> 11% of each run, Pallas kernels for 5% -> 14%
where the time goes in v2:
time: 451 us; the launch traced here: 448 us
  waiting for transfers between devices  221 us (49%)
  Pallas kernels  88.7 us (20%)
  starting transfers between devices  64.5 us (14%)
  local copies, waits for them, and re-layouts  26.2 us (6%)
  other arithmetic  20.1 us (4%)
  between operations  14.6 us (3%)
  matrix products  12.3 us (3%)
    ppermute x47, waiting for transfers between devices, swap(): lax.ppermute(value, axis, [(place, place ^ step) for place in range(size)])  215 us
    ppermute x47, starting transfers between devices, swap(): lax.ppermute(value, axis, [(place, place ^ step) for place in range(size)])  64.2 us
    pallas_call x1, Pallas kernels, attend_back(): pl.pallas_call(backward_kernel, grid_spec=pltpu.PrefetchScalarGridSpec(nu...  18.9 us
    pallas_call x1, Pallas kernels, attend(): pl.pallas_call(forward_kernel, grid_spec=pltpu.PrefetchScalarGridSpec(num...  14.3 us
    pallas_call x1, Pallas kernels, feed_forward(): pl.pallas_call(ff_kernel, grid=(steps,), in_specs=[whole, whole, whole, l...  14.2 us
    pallas_call x2, Pallas kernels, weight_terms(): pl.pallas_call(lambda *refs: weight_kernel(plans, *refs), grid_spec=pltpu...  12.2 us
    pallas_call x1, Pallas kernels, leave(): pl.pallas_call(lambda *refs: leave_kernel(rows, depth * 4, *refs), grid_s...  10.6 us
    unnamed x79, local copies, waits for them, and re-layouts  9.66 us
  transfers between devices with their start and end apart: 51, of which 25 were waited for; matrix products, arithmetic and copies ran while one was open for 11% of the time, Pallas kernels for 14%

profile of v2, /device:TPU:0, one launch (start us, length us, event | category | flops | bytes accessed | tf_op | source)
XLA Modules:
  0.0 447.6 jit_solution(18124468728425832175)
XLA Ops:
  7.2 1.8 pack.1
  9.0 3.0 collective-permute-start
  12.0 2.6 collective-permute-start.1
  14.6 3.2 copy.35
  17.8 1.9 dynamic-slice_bitcast_fusion.1
  19.8 5.6 %collective-permute-done = bf16[200,768]{1,0:T(8,128)(2,1)S(1)} collective-permute-done((bf16[200,768]{1,0:T(8,128)(2,1)}, bf16[200,768]{1,0:T(8,128)(2,1)S(1)}, u32[]{:S(2)}, u32[]{:S(2)}) %collective-permute-start) | collective-permute-done | bytes 307232 | tf_op jit(solution)/shard_map/ppermute | solution.py:63
  25.3 11.3 %collective-permute-done.1 = bf16[200,768]{1,0:T(8,128)(2,1)} collective-permute-done((bf16[200,768]{1,0:T(8,128)(2,1)}, bf16[200,768]{1,0:T(8,128)(2,1)}, u32[]{:S(2)}, u32[]{:S(2)}) %collective-permute-start.1) | collective-permute-done | bytes 307232 | tf_op jit(solution)/shard_map/ppermute | solution.py:63
  37.9 5.8 %collective-permute-start.5 = (bf16[24,3072]{1,0:T(8,128)(2,1)S(1)}, bf16[24,3072]{1,0:T(8,128)(2,1)S(1)}, u32[]{:S(2)}, u32[]{:S(2)}) collective-permute-start(bf16[24,3072]{1,0:T(8,128)(2,1)S(1)} %pad_maximum_fusion.9), channel_id=1, source_target_pairs={{0,8},{8,0},{16,24},{24,16},{1,9},{9,1},{17,25},{25,17},{2,10},{10... | collective-permute-start | bytes 442376 | tf_op jit(solution)/shard_map/ppermute | solution.py:63
  46.1 2.3 collective-permute-done.5
  49.9 6.8 %collective-permute-done.6 = bf16[24,3072]{1,0:T(8,128)(2,1)S(1)} collective-permute-done((bf16[24,3072]{1,0:T(8,128)(2,1)S(1)}, bf16[24,3072]{1,0:T(8,128)(2,1)S(1)}, u32[]{:S(2)}, u32[]{:S(2)}) %collective-permute-start.6) | collective-permute-done | bytes 147488 | tf_op jit(solution)/shard_map/ppermute | solution.py:63
  59.3 3.9 pad_maximum_fusion.refs_1_
  63.1 12.4 %collective-permute-done.3.refs_3_ = bf16[4,200,768]{2,1,0:T(8,128)(2,1)S(1)} collective-permute-done((bf16[4,200,768]{2,1,0:T(8,128)(2,1)S(1)}, bf16[4,200,768]{2,1,0:T(8,128)(2,1)S(1)}, u32[]{:S(2)}, u32[]{:S(2)}) %collective-permute-start.3) | collective-permute-done | bytes 1228832 | tf_op jit(solution)/shard_map/ppermute | solution.py:63
  78.4 1.6 collective-permute-start.11
  82.0 9.1 %collective-permute-done.10.refs_5_ = bf16[4,96,768]{2,1,0:T(8,128)(2,1)S(1)} collective-permute-done((bf16[4,96,768]{2,1,0:T(8,128)(2,1)S(1)}, bf16[4,96,768]{2,1,0:T(8,128)(2,1)S(1)}, u32[]{:S(2)}, u32[]{:S(2)}) %collective-permute-start.10) | collective-permute-done | bytes 589856 | tf_op jit(solution)/shard_map/ppermute | solution.py:63
  91.9 1.8 collective-permute-start.24
  93.7 14.3 %collective-permute-start.25 = (bf16[192,768]{1,0:T(8,128)(2,1)S(1)}, bf16[192,768]{1,0:T(8,128)(2,1)}, u32[]{:S(2)}, u32[]{:S(2)}) collective-permute-start(bf16[192,768]{1,0:T(8,128)(2,1)S(1)} %slice_dynamic-update-slice_fusion), channel_id=1, source_target_pairs={{0,16},{8,24},{16,0},{24,8},{1,17},{9,25},{17,1},{25,9},{2,18},{10... | collective-permute-start | bytes 884744 | tf_op jit(solution)/shard_map/ppermute | solution.py:63
  108.0 12.2 %collective-permute-done.25 = bf16[192,768]{1,0:T(8,128)(2,1)} collective-permute-done((bf16[192,768]{1,0:T(8,128)(2,1)S(1)}, bf16[192,768]{1,0:T(8,128)(2,1)}, u32[]{:S(2)}, u32[]{:S(2)}) %collective-permute-start.25) | collective-permute-done | bytes 294944 | tf_op jit(solution)/shard_map/ppermute | solution.py:63
  124.5 8.6 %enter.1 = f32[256,768]{1,0:T(8,128)} custom-call(s32[17]{0:T(128)} %pad_add_fusion.refs_0_, bf16[256,6144]{1,0:T(8,128)(2,1)} %bitcast.191, bf16[4,200,768]{2,1,0:T(8,128)(2,1)} %copy-done.7, bf16[4,200,768]{2,1,0:T(8,128)(2,1)} %copy-done.8, bf16[4,200,768]{2,1,0:T(8,128)(2,1)} %collective-permute-done.4.refs_4_, bf16[4,96,768]{2,1,0:T(8,128)(2,1)} %copy-done.16, ...), custom_call_target="tpu_custom_call" | custom-call | tf_op jit(solution)/shard_map/enter/pallas_call | solution.py:365
  140.3 3.7 convolution_convert_fusion
  145.7 1.6 collective-permute-start.16
  147.3 27.6 %collective-permute-done.17.refs_2_.refs_10_ = bf16[2,128,1536]{2,1,0:T(8,128)(2,1)S(1)} collective-permute-done((bf16[2,128,1536]{2,1,0:T(8,128)(2,1)}, bf16[2,128,1536]{2,1,0:T(8,128)(2,1)S(1)}, u32[]{:S(2)}, u32[]{:S(2)}) %collective-permute-start.17) | collective-permute-done | bytes 786464 | tf_op jit(solution)/shard_map/ppermute | solution.py:63
  177.7 17.2 %collective-permute-done.18 = bf16[1,128,1536]{2,1,0:T(8,128)(2,1)S(1)} collective-permute-done((bf16[1,128,1536]{2,1,0:T(8,128)(2,1)S(1)}, bf16[1,128,1536]{2,1,0:T(8,128)(2,1)S(1)}, u32[]{:S(2)}, u32[]{:S(2)}) %collective-permute-start.18) | collective-permute-done | bytes 393248 | tf_op jit(solution)/shard_map/ppermute | solution.py:63
  194.9 1.6 collective-permute-done.19
  199.1 14.3 %shard_map.271 = (bf16[2,128,768]{2,1,0:T(8,128)(2,1)}, f32[2,6,1,256]{3,2,1,0:T(1,128)}) custom-call(s32[9]{0:T(128)} %add_multiply_fusion.places, bf16[2,128,2304]{2,1,0:T(8,128)(2,1)} %bitcast.181, bf16[2,128,2304]{2,1,0:T(8,128)(2,1)} %bitcast.182, bf16[2,128,1536]{2,1,0:T(8,128)(2,1)} %copy-done.5, bf16[2,128,1536]{2,1,0:T(8,128)(2,1)} %copy-done.4, ...), custom_call_target="tpu_custom_call" | custom-call | tf_op jit(solution)/shard_map/pallas_call | solution.py:168
  213.4 2.0 fusion.33
  216.6 14.2 %feed_forward.1 = (bf16[256,768]{1,0:T(8,128)(2,1)}, f32[256,768]{1,0:T(8,128)}, f32[4,1,768]{2,1,0:T(1,128)}, bf16[32,192,768]{2,1,0:T(8,128)(2,1)}) custom-call(bf16[256,768]{1,0:T(8,128)(2,1)} %add_convert_fusion.5.a_ref, bf16[256,768]{1,0:T(8,128)(2,1)} %bitcast.197, f32[256,768]{1,0:T(8,128)} %copy-done.1, ...), custom_call_target="tpu_custom_call" | custom-call | tf_op jit(solution)/shard_map/feed_forward/pallas_call | solution.py:517
  232.9 2.7 convolution_convert_fusion.1
  235.6 18.9 %shard_map.272 = (bf16[2,128,768]{2,1,0:T(8,128)(2,1)}, bf16[4,2,128,768]{3,2,1,0:T(8,128)(2,1)}, bf16[4,2,128,768]{3,2,1,0:T(8,128)(2,1)}, bf16[4,2,128,768]{3,2,1,0:T(8,128)(2,1)}, bf16[4,2,128,768]{3,2,1,0:T(8,128)(2,1)}) custom-call(s32[9]{0:T(128)} %add_multiply_fusion.places, bf16[2,128,2304]{2,1,0:T(8,128)(2,1)} %bitcast.184, ...), custom_call_target="tpu_custom_call" | custom-call | tf_op jit(solution)/shard_map/pallas_call | solution.py:190
  255.1 3.1 collective-permute-done.27
  261.6 35.1 %collective-permute-done.28 = bf16[2,2,128,768]{3,2,1,0:T(8,128)(2,1)S(1)} collective-permute-done((bf16[2,2,128,768]{3,2,1,0:T(8,128)(2,1)S(1)}, bf16[2,2,128,768]{3,2,1,0:T(8,128)(2,1)S(1)}, u32[]{:S(2)}, u32[]{:S(2)}) %collective-permute-start.28) | collective-permute-done | bytes 786464 | tf_op jit(solution)/shard_map/ppermute | solution.py:63
  299.0 9.6 %collective-permute-done.29 = bf16[2,128,768]{2,1,0:T(8,128)(2,1)S(1)} collective-permute-done((bf16[2,128,768]{2,1,0:T(8,128)(2,1)S(1)}, bf16[2,128,768]{2,1,0:T(8,128)(2,1)S(1)}, u32[]{:S(2)}, u32[]{:S(2)}) %collective-permute-start.29) | collective-permute-done | bytes 393248 | tf_op jit(solution)/shard_map/ppermute | solution.py:63
  310.0 3.7 multiply_reduce_fusion.1
  317.1 6.1 %weight_terms.2 = (bf16[2,4,192,384]{3,2,1,0:T(8,128)(2,1)}, bf16[2,4,192,384]{3,2,1,0:T(8,128)(2,1)}) custom-call(s32[17]{0:T(128)} %pad_add_fusion.refs_0_, bf16[16,192,512]{2,1,0:T(8,128)(2,1)} %pad_maximum_fusion.refs_1_, bf16[512,768]{1,0:T(8,128)(2,1)} %pad_maximum_fusion.6.refs_2_), custom_call_target="tpu_custom_call" | custom-call | tf_op jit(solution)/shard_map/weight_terms/pallas_call | solution.py:417
  323.2 6.1 %weight_terms.3 = (bf16[2,4,192,384]{3,2,1,0:T(8,128)(2,1)}, bf16[2,4,192,384]{3,2,1,0:T(8,128)(2,1)}) custom-call(s32[17]{0:T(128)} %pad_add_fusion.refs_0_, bf16[16,192,512]{2,1,0:T(8,128)(2,1)} %pad_maximum_fusion.refs_1_, bf16[512,768]{1,0:T(8,128)(2,1)} %pad_maximum_fusion.6.refs_2_), custom_call_target="tpu_custom_call" | custom-call | tf_op jit(solution)/shard_map/weight_terms/pallas_call | solution.py:417
  329.3 8.2 %device_terms.1 = bf16[32,112,768]{2,1,0:T(8,128)(2,1)} custom-call(bf16[256,768]{1,0:T(8,128)(2,1)} %copy-done.17, bf16[256,2304]{1,0:T(8,128)(2,1)} %bitcast.196, bf16[256,768]{1,0:T(8,128)(2,1)} %bitcast.199, bf16[256,768]{1,0:T(8,128)(2,1)} %copy-done.18, bf16[32,16,768]{2,1,0:T(8,128)(2,1)} %copy-done.13), custom_call_target="tpu_custom_call" | custom-call | tf_op jit(solution)/shard_map/device_terms/pallas_call | solution.py:588
  340.0 1.6 collective-permute-start.36
  341.5 2.4 collective-permute-start.37
  344.4 10.6 %leave.1 = f32[256,6144]{1,0:T(8,128)} custom-call(s32[17]{0:T(128)} %pad_add_fusion.refs_0_, bf16[256,768]{1,0:T(8,128)(2,1)} %copy-done.12, bf16[4,200,768]{2,1,0:T(8,128)(2,1)} %copy-done.7, bf16[4,200,768]{2,1,0:T(8,128)(2,1)} %copy-done.8, bf16[4,200,768]{2,1,0:T(8,128)(2,1)} %collective-permute-done.4.refs_4_, bf16[4,96,768]{2,1,0:T(8,128)(2,1)} %copy-done.16, ...), custom_call_target="tpu_custom_call" | custom-call | tf_op jit(solution)/shard_map/leave/pallas_call | solution.py:383
  355.1 9.9 %collective-permute-done.37 = bf16[192,768]{1,0:T(8,128)(2,1)S(1)} collective-permute-done((bf16[192,768]{1,0:T(8,128)(2,1)S(1)}, bf16[192,768]{1,0:T(8,128)(2,1)S(1)}, u32[]{:S(2)}, u32[]{:S(2)}) %collective-permute-start.37) | collective-permute-done | bytes 294944 | tf_op jit(solution)/shard_map/ppermute | solution.py:63
  365.1 4.4 collective-permute-done.34
  369.5 2.0 collective-permute-done.35
  374.2 19.5 %collective-permute-done.40 = bf16[4,192,384]{2,1,0:T(8,128)(2,1)S(1)} collective-permute-done((bf16[4,192,384]{2,1,0:T(8,128)(2,1)S(1)}, bf16[4,192,384]{2,1,0:T(8,128)(2,1)S(1)}, u32[]{:S(2)}, u32[]{:S(2)}) %collective-permute-start.40) | collective-permute-done | bytes 589856 | tf_op jit(solution)/shard_map/ppermute | solution.py:63
  396.6 2.4 collective-permute-start.42
  401.0 6.4 %reduce-scatter.5.cloned.1.call-done = bf16[4,112,768]{2,1,0:T(8,128)(2,1)} async-done(((bf16[4,896,768]{2,1,0:T(8,128)(2,1)}), bf16[4,112,768]{2,1,0:T(8,128)(2,1)}) %reduce-scatter.5.cloned.1.call-update) | async-done | bytes 688144 | tf_op jit(solution)/shard_map/reduce_scatter | solution.py:224
  410.1 2.4 collective-permute-start.45
  413.0 7.2 %collective-permute-done.42 = bf16[192,768]{1,0:T(8,128)(2,1)} collective-permute-done((bf16[192,768]{1,0:T(8,128)(2,1)S(1)}, bf16[192,768]{1,0:T(8,128)(2,1)}, u32[]{:S(2)}, u32[]{:S(2)}) %collective-permute-start.42) | collective-permute-done | bytes 294944 | tf_op jit(solution)/shard_map/ppermute | solution.py:63
  420.2 2.0 fusion.18
  422.2 15.3 %collective-permute-done.45 = bf16[112,768]{1,0:T(8,128)(2,1)S(1)} collective-permute-done((bf16[112,768]{1,0:T(8,128)(2,1)S(1)}, bf16[112,768]{1,0:T(8,128)(2,1)S(1)}, u32[]{:S(2)}, u32[]{:S(2)}) %collective-permute-start.45) | collective-permute-done | bytes 172064 | tf_op jit(solution)/shard_map/ppermute | solution.py:63
  (245 shorter events, 63.3 us)
Async XLA Ops:
  7.2 133.1 %all-gather.3.cloned.1.call-start = ((), (), s32[]{:S(2)}) async-start(), calls=%async_computation.2 | async-start | bytes 5308416 | tf_op jit(solution)/shard_map/all_gather | solution.py:211
  9.0 16.3 %collective-permute-start = (bf16[200,768]{1,0:T(8,128)(2,1)}, bf16[200,768]{1,0:T(8,128)(2,1)S(1)}, u32[]{:S(2)}, u32[]{:S(2)}) collective-permute-start(bf16[200,768]{1,0:T(8,128)(2,1)} %pack.1), channel_id=1, source_target_pairs={{0,8},{8,0},{16,24},{24,16},{1,9},{9,1},{17,25},{25,17},{2,10},{10... | collective-permute-start | bytes 921608 | tf_op jit(solution)/shard_map/ppermute | solution.py:63
  12.0 24.6 %collective-permute-start.1 = (bf16[200,768]{1,0:T(8,128)(2,1)}, bf16[200,768]{1,0:T(8,128)(2,1)}, u32[]{:S(2)}, u32[]{:S(2)}) collective-permute-start(bf16[200,768]{1,0:T(8,128)(2,1)} %pack.1), channel_id=1, source_target_pairs={{0,16},{8,24},{16,0},{24,8},{1,17},{9,25},{17,1},{25,9},{2,18},{10... | collective-permute-start | bytes 921608 | tf_op jit(solution)/shard_map/ppermute | solution.py:63
  14.6 22.0 %collective-permute-start.2 = (bf16[200,768]{1,0:T(8,128)(2,1)}, bf16[200,768]{1,0:T(8,128)(2,1)}, u32[]{:S(2)}, u32[]{:S(2)}) collective-permute-start(bf16[200,768]{1,0:T(8,128)(2,1)} %pack.1), channel_id=1, source_target_pairs={{0,24},{8,16},{16,8},{24,0},{1,25},{9,17},{17,9},{25,1},{2,26},{10... | collective-permute-start | bytes 921608 | tf_op jit(solution)/shard_map/ppermute | solution.py:63
  19.7 39.5 %collective-permute-start.8 = (bf16[16,192,256]{2,1,0:T(8,128)(2,1)}, bf16[16,192,256]{2,1,0:T(8,128)(2,1)}, u32[]{:S(2)}, u32[]{:S(2)}) collective-permute-start(bf16[16,192,256]{2,1,0:T(8,128)(2,1)} %get-tuple-element.104), channel_id=1, source_target_pairs={{0,1},{1,0},{2,3},{3,2},{4,5},{5,4},{6,7},{7,6},{8,9},{9,8},{10,11... | collective-permute-start | bytes 4718600 | tf_op jit(solution)/shard_map/ppermute | solution.py:63
  37.9 10.5 %collective-permute-start.5 = (bf16[24,3072]{1,0:T(8,128)(2,1)S(1)}, bf16[24,3072]{1,0:T(8,128)(2,1)S(1)}, u32[]{:S(2)}, u32[]{:S(2)}) collective-permute-start(bf16[24,3072]{1,0:T(8,128)(2,1)S(1)} %pad_maximum_fusion.9), channel_id=1, source_target_pairs={{0,8},{8,0},{16,24},{24,16},{1,9},{9,1},{17,25},{25,17},{2,10},{10... | collective-permute-start | bytes 442376 | tf_op jit(solution)/shard_map/ppermute | solution.py:63
  43.7 13.0 %collective-permute-start.6 = (bf16[24,3072]{1,0:T(8,128)(2,1)S(1)}, bf16[24,3072]{1,0:T(8,128)(2,1)S(1)}, u32[]{:S(2)}, u32[]{:S(2)}) collective-permute-start(bf16[24,3072]{1,0:T(8,128)(2,1)S(1)} %pad_maximum_fusion.9), channel_id=1, source_target_pairs={{0,16},{8,24},{16,0},{24,8},{1,17},{9,25},{17,1},{25,9},{2,18},{10... | collective-permute-start | bytes 442376 | tf_op jit(solution)/shard_map/ppermute | solution.py:63
  44.7 13.5 %collective-permute-start.7 = (bf16[24,3072]{1,0:T(8,128)(2,1)S(1)}, bf16[24,3072]{1,0:T(8,128)(2,1)S(1)}, u32[]{:S(2)}, u32[]{:S(2)}) collective-permute-start(bf16[24,3072]{1,0:T(8,128)(2,1)S(1)} %pad_maximum_fusion.9), channel_id=1, source_target_pairs={{0,24},{8,16},{16,8},{24,0},{1,25},{9,17},{17,9},{25,1},{2,26},{10... | collective-permute-start | bytes 442376 | tf_op jit(solution)/shard_map/ppermute | solution.py:63
  46.1 17.0 %collective-permute-start.9 = (bf16[4,200,768]{2,1,0:T(8,128)(2,1)S(1)}, bf16[4,200,768]{2,1,0:T(8,128)(2,1)}, u32[]{:S(2)}, u32[]{:S(2)}) collective-permute-start(bf16[4,200,768]{2,1,0:T(8,128)(2,1)S(1)} %pad_maximum_fusion.2.refs_2_), channel_id=1, source_target_pairs={{0,1},{1,0},{2,3},{3,2},{4,5},{5,4},{6,7},{7,6},{8,9},{9,8},{10,11... | collective-permute-start | bytes 3686408 | tf_op jit(solution)/shard_map/ppermute | solution.py:63
  48.4 27.2 %collective-permute-start.3 = (bf16[4,200,768]{2,1,0:T(8,128)(2,1)S(1)}, bf16[4,200,768]{2,1,0:T(8,128)(2,1)S(1)}, u32[]{:S(2)}, u32[]{:S(2)}) collective-permute-start(bf16[4,200,768]{2,1,0:T(8,128)(2,1)S(1)} %pad_maximum_fusion.2.refs_2_), channel_id=1, source_target_pairs={{0,2},{2,0},{1,3},{3,1},{4,6},{6,4},{5,7},{7,5},{8,10},{10,8},{9,1... | collective-permute-start | bytes 3686408 | tf_op jit(solution)/shard_map/ppermute | solution.py:63
  56.7 20.4 %collective-permute-start.4 = (bf16[4,200,768]{2,1,0:T(8,128)(2,1)S(1)}, bf16[4,200,768]{2,1,0:T(8,128)(2,1)}, u32[]{:S(2)}, u32[]{:S(2)}) collective-permute-start(bf16[4,200,768]{2,1,0:T(8,128)(2,1)S(1)} %pad_maximum_fusion.2.refs_2_), channel_id=1, source_target_pairs={{0,4},{4,0},{1,5},{5,1},{2,6},{6,2},{3,7},{7,3},{8,12},{12,8},{9,1... | collective-permute-start | bytes 3686408 | tf_op jit(solution)/shard_map/ppermute | solution.py:63
  77.1 139.5 %all-gather.5.cloned.1.call-start = ((), (), s32[]{:S(2)}) async-start(), calls=%async_computation.3 | async-start | bytes 10616832 | tf_op jit(solution)/shard_map/all_gather | solution.py:211
  78.4 12.7 %collective-permute-start.11 = (bf16[4,104,768]{2,1,0:T(8,128)(2,1)S(1)}, bf16[4,104,768]{2,1,0:T(8,128)(2,1)S(1)}, u32[]{:S(2)}, u32[]{:S(2)}) collective-permute-start(bf16[4,104,768]{2,1,0:T(8,128)(2,1)S(1)} %slice.278), channel_id=1, source_target_pairs={{0,4},{4,0},{1,5},{5,1},{2,6},{6,2},{3,7},{7,3},{8,12},{12,8},{9,1... | collective-permute-start | bytes 1916936 | tf_op jit(solution)/shard_map/ppermute | solution.py:63
  79.9 11.1 %collective-permute-start.10 = (bf16[4,96,768]{2,1,0:T(8,128)(2,1)S(1)}, bf16[4,96,768]{2,1,0:T(8,128)(2,1)S(1)}, u32[]{:S(2)}, u32[]{:S(2)}) collective-permute-start(bf16[4,96,768]{2,1,0:T(8,128)(2,1)S(1)} %slice.277), channel_id=1, source_target_pairs={{0,2},{2,0},{1,3},{3,1},{4,6},{6,4},{5,7},{7,5},{8,10},{10,8},{9,1... | collective-permute-start | bytes 1769480 | tf_op jit(solution)/shard_map/ppermute | solution.py:63
  81.4 42.0 %collective-permute-start.12 = (bf16[4,200,768]{2,1,0:T(8,128)(2,1)S(1)}, bf16[4,200,768]{2,1,0:T(8,128)(2,1)S(1)}, u32[]{:S(2)}, u32[]{:S(2)}) collective-permute-start(bf16[4,200,768]{2,1,0:T(8,128)(2,1)S(1)} %collective-permute-done.3.refs_3_), channel_id=1, source_target_pairs={{0,1},{1,0},{2,3},{3,2},{4,5},{5,4},{6,7},{7,6},{8,9},{9,8},{10,11... | collective-permute-start | bytes 3686408 | tf_op jit(solution)/shard_map/ppermute | solution.py:63
  81.5 42.0 %collective-permute-start.13 = (bf16[4,200,768]{2,1,0:T(8,128)(2,1)}, bf16[4,200,768]{2,1,0:T(8,128)(2,1)}, u32[]{:S(2)}, u32[]{:S(2)}) collective-permute-start(bf16[4,200,768]{2,1,0:T(8,128)(2,1)} %collective-permute-done.4.refs_4_), channel_id=1, source_target_pairs={{0,1},{1,0},{2,3},{3,2},{4,5},{5,4},{6,7},{7,6},{8,9},{9,8},{10,11... | collective-permute-start | bytes 3686408 | tf_op jit(solution)/shard_map/ppermute | solution.py:63
  91.9 16.1 %collective-permute-start.24 = (bf16[192,768]{1,0:T(8,128)(2,1)S(1)}, bf16[192,768]{1,0:T(8,128)(2,1)}, u32[]{:S(2)}, u32[]{:S(2)}) collective-permute-start(bf16[192,768]{1,0:T(8,128)(2,1)S(1)} %slice_dynamic-update-slice_fusion), channel_id=1, source_target_pairs={{0,8},{8,0},{16,24},{24,16},{1,9},{9,1},{17,25},{25,17},{2,10},{10... | collective-permute-start | bytes 884744 | tf_op jit(solution)/shard_map/ppermute | solution.py:63
  93.7 26.5 %collective-permute-start.25 = (bf16[192,768]{1,0:T(8,128)(2,1)S(1)}, bf16[192,768]{1,0:T(8,128)(2,1)}, u32[]{:S(2)}, u32[]{:S(2)}) collective-permute-start(bf16[192,768]{1,0:T(8,128)(2,1)S(1)} %slice_dynamic-update-slice_fusion), channel_id=1, source_target_pairs={{0,16},{8,24},{16,0},{24,8},{1,17},{9,25},{17,1},{25,9},{2,18},{10... | collective-permute-start | bytes 884744 | tf_op jit(solution)/shard_map/ppermute | solution.py:63
  108.0 12.8 %collective-permute-start.26 = (bf16[192,768]{1,0:T(8,128)(2,1)S(1)}, bf16[192,768]{1,0:T(8,128)(2,1)}, u32[]{:S(2)}, u32[]{:S(2)}) collective-permute-start(bf16[192,768]{1,0:T(8,128)(2,1)S(1)} %slice_dynamic-update-slice_fusion), channel_id=1, source_target_pairs={{0,24},{8,16},{16,8},{24,0},{1,25},{9,17},{17,9},{25,1},{2,26},{10... | collective-permute-start | bytes 884744 | tf_op jit(solution)/shard_map/ppermute | solution.py:63
  108.0 15.5 %collective-permute-start.14 = (bf16[4,96,768]{2,1,0:T(8,128)(2,1)}, bf16[4,96,768]{2,1,0:T(8,128)(2,1)}, u32[]{:S(2)}, u32[]{:S(2)}) collective-permute-start(bf16[4,96,768]{2,1,0:T(8,128)(2,1)} %copy-done.16), channel_id=1, source_target_pairs={{0,1},{1,0},{2,3},{3,2},{4,5},{5,4},{6,7},{7,6},{8,9},{9,8},{10,11... | collective-permute-start | bytes 1769480 | tf_op jit(solution)/shard_map/ppermute | solution.py:63
  133.1 196.2 %reduce-scatter.3.cloned.1.call-start = ((), (), s32[]{:S(2)}) async-start(), calls=%async_computation.4 | async-start | bytes 10616832 | tf_op jit(solution)/shard_map/reduce_scatter | solution.py:224
  145.1 29.9 %collective-permute-start.17 = (bf16[2,128,1536]{2,1,0:T(8,128)(2,1)}, bf16[2,128,1536]{2,1,0:T(8,128)(2,1)S(1)}, u32[]{:S(2)}, u32[]{:S(2)}) collective-permute-start(bf16[2,128,1536]{2,1,0:T(8,128)(2,1)} %slice.346), channel_id=1, source_target_pairs={{0,4},{4,0},{1,5},{5,1},{2,6},{6,2},{3,7},{7,3},{8,12},{12,8},{9,1... | collective-permute-start | bytes 2359304 | tf_op jit(solution)/shard_map/ppermute | solution.py:63
  145.7 30.9 %collective-permute-start.16 = (bf16[2,128,1536]{2,1,0:T(8,128)(2,1)}, bf16[2,128,1536]{2,1,0:T(8,128)(2,1)S(1)}, u32[]{:S(2)}, u32[]{:S(2)}) collective-permute-start(bf16[2,128,1536]{2,1,0:T(8,128)(2,1)} %slice.346), channel_id=1, source_target_pairs={{0,2},{2,0},{1,3},{3,1},{4,6},{6,4},{5,7},{7,5},{8,10},{10,8},{9,1... | collective-permute-start | bytes 2359304 | tf_op jit(solution)/shard_map/ppermute | solution.py:63
  175.0 19.9 %collective-permute-start.18 = (bf16[1,128,1536]{2,1,0:T(8,128)(2,1)S(1)}, bf16[1,128,1536]{2,1,0:T(8,128)(2,1)S(1)}, u32[]{:S(2)}, u32[]{:S(2)}) collective-permute-start(bf16[1,128,1536]{2,1,0:T(8,128)(2,1)S(1)} %slice.347), channel_id=1, source_target_pairs={{0,2},{2,0},{1,3},{3,1},{4,6},{6,4},{5,7},{7,5},{8,10},{10,8},{9,1... | collective-permute-start | bytes 1179656 | tf_op jit(solution)/shard_map/ppermute | solution.py:63
  176.6 20.0 %collective-permute-start.19 = (bf16[1,128,1536]{2,1,0:T(8,128)(2,1)S(1)}, bf16[1,128,1536]{2,1,0:T(8,128)(2,1)S(1)}, u32[]{:S(2)}, u32[]{:S(2)}) collective-permute-start(bf16[1,128,1536]{2,1,0:T(8,128)(2,1)S(1)} %slice.348), channel_id=1, source_target_pairs={{0,4},{4,0},{1,5},{5,1},{2,6},{6,2},{3,7},{7,3},{8,12},{12,8},{9,1... | collective-permute-start | bytes 1179656 | tf_op jit(solution)/shard_map/ppermute | solution.py:63
  177.2 21.8 %collective-permute-start.20 = (bf16[2,128,1536]{2,1,0:T(8,128)(2,1)}, bf16[2,128,1536]{2,1,0:T(8,128)(2,1)}, u32[]{:S(2)}, u32[]{:S(2)}) collective-permute-start(bf16[2,128,1536]{2,1,0:T(8,128)(2,1)} %slice.346), channel_id=1, source_target_pairs={{0,1},{1,0},{2,3},{3,2},{4,5},{5,4},{6,7},{7,6},{8,9},{9,8},{10,11... | collective-permute-start | bytes 2359304 | tf_op jit(solution)/shard_map/ppermute | solution.py:63
  177.2 21.8 %collective-permute-start.21 = (bf16[2,128,1536]{2,1,0:T(8,128)(2,1)S(1)}, bf16[2,128,1536]{2,1,0:T(8,128)(2,1)}, u32[]{:S(2)}, u32[]{:S(2)}) collective-permute-start(bf16[2,128,1536]{2,1,0:T(8,128)(2,1)S(1)} %collective-permute-done.16.refs_1_.refs_9_), channel_id=1, source_target_pairs={{0,1},{1,0},{2,3},{3,2},{4,5},{5,4},{6,7},{7,6},{8,9},{9,8},{10,11... | collective-permute-start | bytes 2359304 | tf_op jit(solution)/shard_map/ppermute | solution.py:63
  177.7 21.3 %collective-permute-start.22 = (bf16[2,128,1536]{2,1,0:T(8,128)(2,1)S(1)}, bf16[2,128,1536]{2,1,0:T(8,128)(2,1)}, u32[]{:S(2)}, u32[]{:S(2)}) collective-permute-start(bf16[2,128,1536]{2,1,0:T(8,128)(2,1)S(1)} %collective-permute-done.17.refs_2_.refs_10_), channel_id=1, source_target_pairs={{0,1},{1,0},{2,3},{3,2},{4,5},{5,4},{6,7},{7,6},{8,9},{9,8},{10,11... | collective-permute-start | bytes 2359304 | tf_op jit(solution)/shard_map/ppermute | solution.py:63
  230.8 176.6 %reduce-scatter.5.cloned.1.call-start = ((), (), s32[]{:S(2)}) async-start(), calls=%async_computation.5 | async-start | bytes 6193152 | tf_op jit(solution)/shard_map/reduce_scatter | solution.py:224
  254.5 3.7 collective-permute-start.27
  254.8 5.6 %collective-permute-start.30 = (bf16[4,2,128,768]{3,2,1,0:T(8,128)(2,1)}, bf16[4,2,128,768]{3,2,1,0:T(8,128)(2,1)S(1)}, u32[]{:S(2)}, u32[]{:S(2)}) collective-permute-start(bf16[4,2,128,768]{3,2,1,0:T(8,128)(2,1)} %get-tuple-element.79), channel_id=1, source_target_pairs={{0,1},{1,0},{2,3},{3,2},{4,5},{5,4},{6,7},{7,6},{8,9},{9,8},{10,11... | collective-permute-start | bytes 4718600 | tf_op jit(solution)/shard_map/ppermute | solution.py:63
  259.6 37.1 %collective-permute-start.28 = (bf16[2,2,128,768]{3,2,1,0:T(8,128)(2,1)S(1)}, bf16[2,2,128,768]{3,2,1,0:T(8,128)(2,1)S(1)}, u32[]{:S(2)}, u32[]{:S(2)}) collective-permute-start(bf16[2,2,128,768]{3,2,1,0:T(8,128)(2,1)S(1)} %fusion.7), channel_id=1, source_target_pairs={{0,2},{2,0},{1,3},{3,1},{4,6},{6,4},{5,7},{7,5},{8,10},{10,8},{9,1... | collective-permute-start | bytes 2359304 | tf_op jit(solution)/shard_map/ppermute | solution.py:63
  260.7 37.0 %collective-permute-start.31 = (bf16[2,2,128,768]{3,2,1,0:T(8,128)(2,1)S(1)}, bf16[2,2,128,768]{3,2,1,0:T(8,128)(2,1)S(1)}, u32[]{:S(2)}, u32[]{:S(2)}) collective-permute-start(bf16[2,2,128,768]{3,2,1,0:T(8,128)(2,1)S(1)} %add_convert_fusion), channel_id=1, source_target_pairs={{0,4},{4,0},{1,5},{5,1},{2,6},{6,2},{3,7},{7,3},{8,12},{12,8},{9,1... | collective-permute-start | bytes 2359304 | tf_op jit(solution)/shard_map/ppermute | solution.py:63
  296.8 11.8 %collective-permute-start.29 = (bf16[2,128,768]{2,1,0:T(8,128)(2,1)S(1)}, bf16[2,128,768]{2,1,0:T(8,128)(2,1)S(1)}, u32[]{:S(2)}, u32[]{:S(2)}) collective-permute-start(bf16[2,128,768]{2,1,0:T(8,128)(2,1)S(1)} %fusion.8), channel_id=1, source_target_pairs={{0,4},{4,0},{1,5},{5,1},{2,6},{6,2},{3,7},{7,3},{8,12},{12,8},{9,1... | collective-permute-start | bytes 1179656 | tf_op jit(solution)/shard_map/ppermute | solution.py:63
  297.9 10.9 %collective-permute-start.32 = (bf16[2,128,768]{2,1,0:T(8,128)(2,1)S(1)}, bf16[2,128,768]{2,1,0:T(8,128)(2,1)S(1)}, u32[]{:S(2)}, u32[]{:S(2)}) collective-permute-start(bf16[2,128,768]{2,1,0:T(8,128)(2,1)S(1)} %fusion.21), channel_id=1, source_target_pairs={{0,2},{2,0},{1,3},{3,1},{4,6},{6,4},{5,7},{7,5},{8,10},{10,8},{9,1... | collective-permute-start | bytes 1179656 | tf_op jit(solution)/shard_map/ppermute | solution.py:63
  337.5 32.0 %collective-permute-start.34 = (bf16[2,4,192,384]{3,2,1,0:T(8,128)(2,1)}, bf16[2,4,192,384]{3,2,1,0:T(8,128)(2,1)S(1)}, u32[]{:S(2)}, u32[]{:S(2)}) collective-permute-start(bf16[2,4,192,384]{3,2,1,0:T(8,128)(2,1)} %get-tuple-element.81), channel_id=1, source_target_pairs={{0,2},{2,0},{1,3},{3,1},{4,6},{6,4},{5,7},{7,5},{8,10},{10,8},{9,1... | collective-permute-start | bytes 3538952 | tf_op jit(solution)/shard_map/ppermute | solution.py:63
  339.0 32.4 %collective-permute-start.35 = (bf16[2,4,192,384]{3,2,1,0:T(8,128)(2,1)S(1)}, bf16[2,4,192,384]{3,2,1,0:T(8,128)(2,1)S(1)}, u32[]{:S(2)}, u32[]{:S(2)}) collective-permute-start(bf16[2,4,192,384]{3,2,1,0:T(8,128)(2,1)S(1)} %copy-done.31), channel_id=1, source_target_pairs={{0,4},{4,0},{1,5},{5,1},{2,6},{6,2},{3,7},{7,3},{8,12},{12,8},{9,1... | collective-permute-start | bytes 3538952 | tf_op jit(solution)/shard_map/ppermute | solution.py:63
  340.0 15.1 %collective-permute-start.36 = (bf16[192,768]{1,0:T(8,128)(2,1)S(1)}, bf16[192,768]{1,0:T(8,128)(2,1)S(1)}, u32[]{:S(2)}, u32[]{:S(2)}) collective-permute-start(bf16[192,768]{1,0:T(8,128)(2,1)S(1)} %get-tuple-element.108), channel_id=1, source_target_pairs={{0,8},{8,0},{16,24},{24,16},{1,9},{9,1},{17,25},{25,17},{2,10},{10... | collective-permute-start | bytes 884744 | tf_op jit(solution)/shard_map/ppermute | solution.py:63
  341.5 23.4 %collective-permute-start.37 = (bf16[192,768]{1,0:T(8,128)(2,1)S(1)}, bf16[192,768]{1,0:T(8,128)(2,1)S(1)}, u32[]{:S(2)}, u32[]{:S(2)}) collective-permute-start(bf16[192,768]{1,0:T(8,128)(2,1)S(1)} %get-tuple-element.110), channel_id=1, source_target_pairs={{0,16},{8,24},{16,0},{24,8},{1,17},{9,25},{17,1},{25,9},{2,18},{10... | collective-permute-start | bytes 884744 | tf_op jit(solution)/shard_map/ppermute | solution.py:63
  343.9 21.0 %collective-permute-start.38 = (bf16[192,768]{1,0:T(8,128)(2,1)S(1)}, bf16[192,768]{1,0:T(8,128)(2,1)S(1)}, u32[]{:S(2)}, u32[]{:S(2)}) collective-permute-start(bf16[192,768]{1,0:T(8,128)(2,1)S(1)} %get-tuple-element.109), channel_id=1, source_target_pairs={{0,24},{8,16},{16,8},{24,0},{1,25},{9,17},{17,9},{25,1},{2,26},{10... | collective-permute-start | bytes 884744 | tf_op jit(solution)/shard_map/ppermute | solution.py:63
  371.6 22.1 %collective-permute-start.40 = (bf16[4,192,384]{2,1,0:T(8,128)(2,1)S(1)}, bf16[4,192,384]{2,1,0:T(8,128)(2,1)S(1)}, u32[]{:S(2)}, u32[]{:S(2)}) collective-permute-start(bf16[4,192,384]{2,1,0:T(8,128)(2,1)S(1)} %fusion.13), channel_id=1, source_target_pairs={{0,2},{2,0},{1,3},{3,1},{4,6},{6,4},{5,7},{7,5},{8,10},{10,8},{9,1... | collective-permute-start | bytes 1769480 | tf_op jit(solution)/shard_map/ppermute | solution.py:63
  373.0 21.7 %collective-permute-start.39 = (bf16[4,192,384]{2,1,0:T(8,128)(2,1)S(1)}, bf16[4,192,384]{2,1,0:T(8,128)(2,1)S(1)}, u32[]{:S(2)}, u32[]{:S(2)}) collective-permute-start(bf16[4,192,384]{2,1,0:T(8,128)(2,1)S(1)} %fusion.12), channel_id=1, source_target_pairs={{0,4},{4,0},{1,5},{5,1},{2,6},{6,2},{3,7},{7,3},{8,12},{12,8},{9,1... | collective-permute-start | bytes 1769480 | tf_op jit(solution)/shard_map/ppermute | solution.py:63
  395.1 17.4 %collective-permute-start.41 = (bf16[192,768]{1,0:T(8,128)(2,1)S(1)}, bf16[192,768]{1,0:T(8,128)(2,1)S(1)}, u32[]{:S(2)}, u32[]{:S(2)}) collective-permute-start(bf16[192,768]{1,0:T(8,128)(2,1)S(1)} %get-tuple-element.105), channel_id=1, source_target_pairs={{0,8},{8,0},{16,24},{24,16},{1,9},{9,1},{17,25},{25,17},{2,10},{10... | collective-permute-start | bytes 884744 | tf_op jit(solution)/shard_map/ppermute | solution.py:63
  396.6 23.6 %collective-permute-start.42 = (bf16[192,768]{1,0:T(8,128)(2,1)S(1)}, bf16[192,768]{1,0:T(8,128)(2,1)}, u32[]{:S(2)}, u32[]{:S(2)}) collective-permute-start(bf16[192,768]{1,0:T(8,128)(2,1)S(1)} %get-tuple-element.107), channel_id=1, source_target_pairs={{0,16},{8,24},{16,0},{24,8},{1,17},{9,25},{17,1},{25,9},{2,18},{10... | collective-permute-start | bytes 884744 | tf_op jit(solution)/shard_map/ppermute | solution.py:63
  399.0 21.2 %collective-permute-start.43 = (bf16[192,768]{1,0:T(8,128)(2,1)S(1)}, bf16[192,768]{1,0:T(8,128)(2,1)}, u32[]{:S(2)}, u32[]{:S(2)}) collective-permute-start(bf16[192,768]{1,0:T(8,128)(2,1)S(1)} %get-tuple-element.106), channel_id=1, source_target_pairs={{0,24},{8,16},{16,8},{24,0},{1,25},{9,17},{17,9},{25,1},{2,26},{10... | collective-permute-start | bytes 884744 | tf_op jit(solution)/shard_map/ppermute | solution.py:63
  408.5 13.7 %collective-permute-start.44 = (bf16[112,768]{1,0:T(8,128)(2,1)S(1)}, bf16[112,768]{1,0:T(8,128)(2,1)S(1)}, u32[]{:S(2)}, u32[]{:S(2)}) collective-permute-start(bf16[112,768]{1,0:T(8,128)(2,1)S(1)} %get-tuple-element.115), channel_id=1, source_target_pairs={{0,8},{8,0},{16,24},{24,16},{1,9},{9,1},{17,25},{25,17},{2,10},{10... | collective-permute-start | bytes 516104 | tf_op jit(solution)/shard_map/ppermute | solution.py:63
  410.1 27.4 %collective-permute-start.45 = (bf16[112,768]{1,0:T(8,128)(2,1)S(1)}, bf16[112,768]{1,0:T(8,128)(2,1)S(1)}, u32[]{:S(2)}, u32[]{:S(2)}) collective-permute-start(bf16[112,768]{1,0:T(8,128)(2,1)S(1)} %get-tuple-element.117), channel_id=1, source_target_pairs={{0,16},{8,24},{16,0},{24,8},{1,17},{9,25},{17,1},{25,9},{2,18},{10... | collective-permute-start | bytes 516104 | tf_op jit(solution)/shard_map/ppermute | solution.py:63
  412.5 25.0 %collective-permute-start.46 = (bf16[112,768]{1,0:T(8,128)(2,1)S(1)}, bf16[112,768]{1,0:T(8,128)(2,1)S(1)}, u32[]{:S(2)}, u32[]{:S(2)}) collective-permute-start(bf16[112,768]{1,0:T(8,128)(2,1)S(1)} %get-tuple-element.116), channel_id=1, source_target_pairs={{0,24},{8,16},{16,8},{24,0},{1,25},{9,17},{17,9},{25,1},{2,26},{10... | collective-permute-start | bytes 516104 | tf_op jit(solution)/shard_map/ppermute | solution.py:63
  (36 other events, 349.5 us)
Sparse Core Ops, SparseCore 0:
  77.2 48.2 all-gather.2
  133.2 79.5 all-gather.4
  230.9 94.7 reduce-scatter.2
  337.6 69.7 reduce-scatter.4
